TPU v7x, 256 devices: a whole 4x4x8 slice. The times are simulated.
256 devices in a mesh: src: 2 (over z_hi), gx: 8 (over z_lo, core), gy: 16 (over y, x).
Axes of the slice: x: 4, y: 4, z: 8 (z_hi: 2, z_lo: 4; z = z_hi * 4 + z_lo), core: 2. Of those that a mesh axis runs over, the one named last changes fastest.
Arguments:
- forward_state: float32 [4, 6, 128, 65536], P('src', None, 'gx', 'gy'), may hold values from -6 to 6
- adjoint_state: float32 [4, 6, 128, 65536], P('src', None, 'gx', 'gy'), may hold values from -6 to 6
- permittivity: float32 [128, 65536], P('gx', 'gy'), may hold values from 1 to 3
- waveform: float32 [4, 4], P('src'), may hold values from -8 to 8
- source_cell: int32 [4, 3], P('src'), may hold values from 0 to 1023, as said below
- block_owner: int32 [32, 256], P('gx', 'gy'), may hold values from -1 to 15, as said below
- block_slot: int32 [32, 256], P('gx', 'gy'), may hold values from -1 to 3, as said below
- owner_rows: int32 [128, 64], P(('gx', 'gy')), may hold values from 0 to 63, as said below
Outputs:
- design_gradient: float32 [8192, 1024], P(('gx', 'gy'), 'src')
Inputs may be any that keep to these rules, and one draw needn't show every extreme that they name: `block_owner`: -1 marks a block outside the design region; otherwise the owner lies in the block's own gx row. The design blocks of one device that go to one owner number at most 4, and some device sends exactly 4 to some owner. `block_slot`: -1 exactly where block_owner is -1; the blocks that one device sends to one owner have distinct slots. `owner_rows`: each row is a permutation of 0 to 63. `source_cell`: each row is a cell (x, y, z) of the grid.
All inputs are finite; a program needn't handle non-finite values.
Results may differ from a plain program's by a relative error of at most 0.0003.
Values sent between devices are 32-bit elements; how exact they have to be, the bound alone decides.
No kernel may reach another device: no remote copies, remote signals or barrier semaphores. Data moves between devices by JAX's collectives and lax.ppermute only.
A program may use at most 128 MiB of HBM per device.

v0:
```python
import jax
import jax.numpy as jnp
from jax import lax
from jax.sharding import PartitionSpec as P

NZ = 64
STEPS = 4
BX = 4
BY = 4
courant = 0.55


def passed_along(shard, axis, by):
    count = lax.axis_size(axis)
    pairs = [(i, i + by) for i in range(count) if 0 <= i + by < count]
    return lax.ppermute(shard, axis, pairs)


def upper_z(values, z_cells):
    zindex = lax.broadcasted_iota(jnp.int32, values.shape, values.ndim - 1) % z_cells
    shifted = jnp.concatenate([values[..., 1:], jnp.zeros_like(values[..., :1])], axis=-1)
    return jnp.where(zindex == z_cells - 1, jnp.zeros_like(shifted), shifted)


def lower_z(values, z_cells):
    zindex = lax.broadcasted_iota(jnp.int32, values.shape, values.ndim - 1) % z_cells
    shifted = jnp.concatenate([jnp.zeros_like(values[..., :1]), values[..., :-1]], axis=-1)
    return jnp.where(zindex == 0, jnp.zeros_like(shifted), shifted)


def upper_x(values, ghosts):
    return jnp.concatenate([values[..., 1:, :], ghosts], axis=-2)


def lower_x(values, ghosts):
    return jnp.concatenate([ghosts, values[..., :-1, :]], axis=-2)


def upper_y(values, ghosts, z_cells):
    return jnp.concatenate([values[..., z_cells:], ghosts], axis=-1)


def lower_y(values, ghosts, z_cells):
    return jnp.concatenate([ghosts, values[..., :-z_cells]], axis=-1)


def magnetic_update(electric, magnetic, ghost_x, ghost_y, z_cells):
    new_hx = magnetic[0] - courant * (
        upper_y(electric[2], ghost_y[1], z_cells)
        - electric[2]
        - (upper_z(electric[1], z_cells) - electric[1])
    )
    new_hy = magnetic[1] - courant * (
        upper_z(electric[0], z_cells)
        - electric[0]
        - (upper_x(electric[2], ghost_x[1]) - electric[2])
    )
    new_hz = magnetic[2] - courant * (
        upper_x(electric[1], ghost_x[0])
        - electric[1]
        - (upper_y(electric[0], ghost_y[0], z_cells) - electric[0])
    )
    return (new_hx, new_hy, new_hz)


def electric_update(electric, magnetic, ghost_x, ghost_y, factor, z_cells):
    new_ex = electric[0] + factor * (
        magnetic[2]
        - lower_y(magnetic[2], ghost_y[1], z_cells)
        - (magnetic[1] - lower_z(magnetic[1], z_cells))
    )
    new_ey = electric[1] + factor * (
        magnetic[0]
        - lower_z(magnetic[0], z_cells)
        - (magnetic[2] - lower_x(magnetic[2], ghost_x[1]))
    )
    new_ez = electric[2] + factor * (
        magnetic[1]
        - lower_x(magnetic[1], ghost_x[0])
        - (magnetic[0] - lower_y(magnetic[0], ghost_y[0], z_cells))
    )
    return (new_ex, new_ey, new_ez)


def upper_ghosts(electric, z_cells):
    planes = jnp.stack([electric[1][:, :1, :], electric[2][:, :1, :]], axis=1)
    planes = passed_along(planes, "gx", -1)
    strips = jnp.stack([electric[0][..., :z_cells], electric[2][..., :z_cells]], axis=1)
    flat_strips = passed_along(strips.reshape(strips.shape[0], 2, -1), "gy", -1)
    strips = flat_strips.reshape(strips.shape)
    return ((planes[:, 0], planes[:, 1]), (strips[:, 0], strips[:, 1]))


def lower_ghosts(magnetic, z_cells):
    planes = jnp.stack([magnetic[1][:, -1:, :], magnetic[2][:, -1:, :]], axis=1)
    planes = passed_along(planes, "gx", 1)
    strips = jnp.stack([magnetic[0][..., -z_cells:], magnetic[2][..., -z_cells:]], axis=1)
    flat_strips = passed_along(strips.reshape(strips.shape[0], 2, -1), "gy", 1)
    strips = flat_strips.reshape(strips.shape)
    return ((planes[:, 0], planes[:, 1]), (strips[:, 0], strips[:, 1]))


def advance(electric, magnetic, factor, z_cells):
    ghost_x, ghost_y = upper_ghosts(electric, z_cells)
    magnetic = magnetic_update(electric, magnetic, ghost_x, ghost_y, z_cells)
    ghost_x, ghost_y = lower_ghosts(magnetic, z_cells)
    electric = electric_update(electric, magnetic, ghost_x, ghost_y, factor, z_cells)
    return (electric, magnetic)


def per_device(
    forward_state,
    adjoint_state,
    permittivity,
    waveform,
    source_cell,
    block_owner,
    block_slot,
    owner_rows,
):
    cells_x = permittivity.shape[0]
    cells_yz = permittivity.shape[1]
    cells_y = cells_yz // NZ
    factor = courant / permittivity
    x_index = lax.broadcasted_iota(jnp.int32, (cells_x, cells_yz), 0)
    yz_index = lax.broadcasted_iota(jnp.int32, (cells_x, cells_yz), 1)
    local_x = source_cell[:, 0] - lax.axis_index("gx") * cells_x
    local_yz = (source_cell[:, 1] - lax.axis_index("gy") * cells_y) * NZ + source_cell[:, 2]
    beacon = (
        (x_index[None] == local_x[:, None, None]) & (yz_index[None] == local_yz[:, None, None])
    ).astype(jnp.float32)
    density = jnp.zeros((cells_x, cells_yz), jnp.float32)
    electric = (forward_state[:, 0], forward_state[:, 1], forward_state[:, 2])
    magnetic = (forward_state[:, 3], forward_state[:, 4], forward_state[:, 5])
    increments = []
    for step_index in range(STEPS):
        updated, magnetic = advance(electric, magnetic, factor, NZ)
        updated = (
            updated[0],
            updated[1],
            updated[2] + waveform[:, step_index][:, None, None] * beacon,
        )
        increments.append(
            (updated[0] - electric[0], updated[1] - electric[1], updated[2] - electric[2])
        )
        electric = updated
    electric = (adjoint_state[:, 0], adjoint_state[:, 1], adjoint_state[:, 2])
    magnetic = (adjoint_state[:, 3], adjoint_state[:, 4], adjoint_state[:, 5])
    for step_index in range(STEPS):
        electric, magnetic = advance(electric, magnetic, factor, NZ)
        paired = increments[STEPS - 1 - step_index]
        intersection = electric[0] * paired[0] + electric[1] * paired[1] + electric[2] * paired[2]
        density = density + jnp.sum(intersection, axis=0)
    gradient = -density / permittivity
    blocks = (
        gradient.reshape(cells_x // BX, BX, cells_y // BY, BY, NZ)
        .transpose(0, 2, 1, 3, 4)
        .reshape(-1, BX * BY * NZ)
    )
    owners = block_owner.reshape(-1)
    slots = block_slot.reshape(-1)
    peers = lax.axis_size("gy")
    capacity = max(2, (blocks.shape[0] + peers - 1) // peers)
    rows_owned = peers * capacity
    destination = jnp.where(owners >= 0, owners * capacity + slots, rows_owned)
    outgoing = (
        jnp.zeros((rows_owned, blocks.shape[1]), jnp.float32)
        .at[destination]
        .set(blocks, mode="drop")
    )
    sectioned = outgoing.reshape(peers, capacity, 1, -1)
    arrived = lax.all_to_all(
        lax.all_to_all(sectioned, "src", split_axis=3, concat_axis=2, tiled=True),
        "gy",
        split_axis=0,
        concat_axis=0,
        tiled=True,
    )
    arrived = jnp.sum(arrived, axis=2)
    placed = jnp.zeros((rows_owned, arrived.shape[-1]), jnp.float32)
    return placed.at[owner_rows[0]].set(arrived.reshape(rows_owned, -1))


def solution(mesh):
    in_specs = (
        P("src", None, "gx", "gy"),
        P("src", None, "gx", "gy"),
        P("gx", "gy"),
        P("src", None),
        P("src", None),
        P("gx", "gy"),
        P("gx", "gy"),
        P(("gx", "gy"), None),
    )
    out_specs = P(("gx", "gy"), "src")
    return jax.shard_map(
        per_device, mesh=mesh, in_specs=in_specs, out_specs=out_specs, check_vma=False
    )
```

profile of v0, /device:TPU:32, one launch (start us, length us, event | category | flops | bytes accessed | tf_op | source)
XLA Modules:
  0.0 353.1 jit_solution(7784408515119125524)
XLA Ops:
  0.0 1.5 slice_bitcast_fusion.2
  2.3 1.9 collective-permute-start.3
  5.7 1.5 slice_bitcast_fusion.5
  7.9 3.8 %collective-permute-start = (f32[2,2,1,4096]{3,1,2,0:T(2,128)}, f32[2,2,1,4096]{3,1,2,0:T(2,128)}, u32[]{:S(2)}, u32[]{:S(2)}) collective-permute-start(f32[2,2,1,4096]{3,1,2,0:T(2,128)} %pad_maximum_fusion), channel_id=1, source_target_pairs={{16,0},{32,16},{48,32},{64,48},{80,64},{96,80},{112,96},{17,1},{33... | collective-permute-start | bytes 196616 | tf_op jit(solution)/shard_map/ppermute | solution.py:16
  28.9 1.8 fusion.173
  32.5 1.5 fusion.170
  36.8 5.5 %collective-permute-start.5 = (f32[2,2,1024]{2,0,1:T(2,128)}, f32[2,2,1024]{2,0,1:T(2,128)}, u32[]{:S(2)}, u32[]{:S(2)}) collective-permute-start(f32[2,2,1024]{2,0,1:T(2,128)} %pad_maximum_fusion.19), channel_id=1, source_target_pairs={{0,1},{1,2},{2,3},{3,4},{4,5},{5,6},{6,7},{7,8},{8,9},{9,10},{10,1... | collective-permute-start | bytes 49160 | tf_op jit(solution)/shard_map/ppermute | solution.py:16
  43.0 1.9 collective-permute-start.6
  45.0 2.7 fusion.102
  48.5 2.3 collective-permute-start.18
  51.8 3.3 collective-permute-start.2
  59.7 1.7 fusion.43
  69.6 2.4 collective-permute-start.7
  72.1 1.8 collective-permute-done.7
  74.0 2.5 fusion.118
  77.7 4.5 %collective-permute-start.9 = (f32[2,2,1024]{2,0,1:T(2,128)S(1)}, f32[2,2,1024]{2,0,1:T(2,128)S(1)}, u32[]{:S(2)}, u32[]{:S(2)}) collective-permute-start(f32[2,2,1024]{2,0,1:T(2,128)S(1)} %pad_maximum_fusion.21), channel_id=1, source_target_pairs={{0,1},{1,2},{2,3},{3,4},{4,5},{5,6},{6,7},{7,8},{8,9},{9,10},{10,1... | collective-permute-start | bytes 49160 | tf_op jit(solution)/shard_map/ppermute | solution.py:16
  82.4 3.5 collective-permute-start.10
  86.0 2.0 collective-permute-done.10
  88.1 1.5 fusion.184
  97.7 1.5 pad_maximum_fusion.5
  105.0 1.9 collective-permute-start.11
  110.1 3.6 %fusion.126 = (f32[2,16,4096]{2,1,0:T(8,128)S(1)}, f32[2,16,4096]{2,1,0:T(8,128)}, f32[2,16,4096]{2,1,0:T(8,128)S(1)}) fusion(f32[2,16,4096]{2,1,0:T(8,128)} %copy-done.9, f32[2,16,4096]{2,1,0:T(8,128)S(1)} %get-tuple-element.36, f32[2,16,4096]{2,1,0:T(8,128)S(1)} %fusion.184, f32[2,16,64]{2,1,0:T(8,128)S(1)} %get-tuple-element.110, ...), kind=kLoop, calls=%fused_computation.132 | loop fusion | flops 3014656 | bytes 7900928 | tf_op jit(solution)/shard_map/sub | solution.py:48
  114.9 5.1 %collective-permute-start.13 = (f32[2,2,1024]{2,0,1:T(2,128)S(1)}, f32[2,2,1024]{2,0,1:T(2,128)S(1)}, u32[]{:S(2)}, u32[]{:S(2)}) collective-permute-start(f32[2,2,1024]{2,0,1:T(2,128)S(1)} %pad_maximum_fusion.23), channel_id=1, source_target_pairs={{0,1},{1,2},{2,3},{3,4},{4,5},{5,6},{6,7},{7,8},{8,9},{9,10},{10,1... | collective-permute-start | bytes 49160 | tf_op jit(solution)/shard_map/ppermute | solution.py:16
  121.1 3.7 %collective-permute-start.14 = (f32[2,2,1,4096]{3,1,2,0:T(2,128)S(1)}, f32[2,2,1,4096]{3,1,2,0:T(2,128)S(1)}, u32[]{:S(2)}, u32[]{:S(2)}) collective-permute-start(f32[2,2,1,4096]{3,1,2,0:T(2,128)S(1)} %pad_maximum_fusion.6), channel_id=1, source_target_pairs={{0,16},{16,32},{32,48},{48,64},{64,80},{80,96},{96,112},{1,17},{17... | collective-permute-start | bytes 196616 | tf_op jit(solution)/shard_map/ppermute | solution.py:16
  125.0 1.8 collective-permute-done.14
  126.8 1.8 fusion.191
  129.3 2.3 fusion.59
  136.5 1.5 collective-permute-start.16
  145.2 1.9 collective-permute-start.15
  150.3 3.0 fusion.134
  158.9 5.4 %collective-permute-start.17 = (f32[2,2,1024]{2,0,1:T(2,128)S(1)}, f32[2,2,1024]{2,0,1:T(2,128)}, u32[]{:S(2)}, u32[]{:S(2)}) collective-permute-start(f32[2,2,1024]{2,0,1:T(2,128)S(1)} %pad_maximum_fusion.25), channel_id=1, source_target_pairs={{0,1},{1,2},{2,3},{3,4},{4,5},{5,6},{6,7},{7,8},{8,9},{9,10},{10,1... | collective-permute-start | bytes 49160 | tf_op jit(solution)/shard_map/ppermute | solution.py:16
  165.8 3.7 %collective-permute-start.19 = (f32[2,2,1,4096]{3,1,2,0:T(2,128)}, f32[2,2,1,4096]{3,1,2,0:T(2,128)}, u32[]{:S(2)}, u32[]{:S(2)}) collective-permute-start(f32[2,2,1,4096]{3,1,2,0:T(2,128)} %pad_maximum_fusion.9), channel_id=1, source_target_pairs={{0,16},{16,32},{32,48},{48,64},{64,80},{80,96},{96,112},{1,17},{17... | collective-permute-start | bytes 196616 | tf_op jit(solution)/shard_map/ppermute | solution.py:16
  172.7 6.4 %fusion.166 = (f32[16,4096]{1,0:T(8,128)}, f32[2,16,4096]{2,1,0:T(8,128)S(1)}, f32[2,16,4096]{2,1,0:T(8,128)S(1)}, f32[2,16,4096]{2,1,0:T(8,128)S(1)}) fusion(f32[2,16,4096]{2,1,0:T(8,128)} %get-tuple-element.35, f32[2,16,4096]{2,1,0:T(8,128)} %copy-done.48, f32[2,16,4096]{2,1,0:T(8,128)S(1)} %get-tuple-element.34, f32[2,16,4096]{2,1,0:T(8,128)} %copy-done.50, ...), kind=kLoop, calls=%fused_computation.172 | loop fusion | flops 7536640 | bytes 14716440 | tf_op jit(solution)/shard_map/reduce_sum | solution.py:153
  182.5 1.9 slice.1112
  184.4 2.0 slice.1116
  186.5 2.0 slice.1120
  191.4 1.9 collective-permute-start.20
  195.6 4.1 %fusion.142 = (f32[2,16,4096]{2,1,0:T(8,128)S(1)}, f32[2,16,4096]{2,1,0:T(8,128)}, f32[2,16,4096]{2,1,0:T(8,128)S(1)}) fusion(f32[2,16,4096]{2,1,0:T(8,128)} %copy-done.37, f32[2,16,4096]{2,1,0:T(8,128)} %copy-done.33, f32[2,16,4096]{2,1,0:T(8,128)} %copy-done.20, f32[2,16,64]{2,1,0:T(8,128)S(1)} %get-tuple-element.98, f32[2,16,4032]{2,1,0:T(8,128)} %slice.1120, ...), kind=kLoop, calls=%fused_computation.148 | loop fusion | flops 3014656 | bytes 7900928 | tf_op jit(solution)/shard_map/sub | solution.py:48
  200.9 6.7 %collective-permute-start.22 = (f32[2,2,1024]{2,0,1:T(2,128)S(1)}, f32[2,2,1024]{2,0,1:T(2,128)}, u32[]{:S(2)}, u32[]{:S(2)}) collective-permute-start(f32[2,2,1024]{2,0,1:T(2,128)S(1)} %pad_maximum_fusion.27), channel_id=1, source_target_pairs={{0,1},{1,2},{2,3},{3,4},{4,5},{5,6},{6,7},{7,8},{8,9},{9,10},{10,1... | collective-permute-start | bytes 49160 | tf_op jit(solution)/shard_map/ppermute | solution.py:16
  209.3 3.6 %collective-permute-start.23 = (f32[2,2,1,4096]{3,1,2,0:T(2,128)}, f32[2,2,1,4096]{3,1,2,0:T(2,128)S(1)}, u32[]{:S(2)}, u32[]{:S(2)}) collective-permute-start(f32[2,2,1,4096]{3,1,2,0:T(2,128)} %pad_maximum_fusion.11), channel_id=1, source_target_pairs={{0,16},{16,32},{32,48},{48,64},{64,80},{80,96},{96,112},{1,17},{17... | collective-permute-start | bytes 196616 | tf_op jit(solution)/shard_map/ppermute | solution.py:16
  215.1 1.9 fusion.209
  221.7 1.9 slice.1140
  223.6 2.0 slice.1144
  225.6 2.0 slice.1150
  230.6 1.9 collective-permute-start.24
  234.8 4.1 %fusion.150 = (f32[2,16,4096]{2,1,0:T(8,128)S(1)}, f32[2,16,4096]{2,1,0:T(8,128)}, f32[2,16,4096]{2,1,0:T(8,128)S(1)}) fusion(f32[2,16,4096]{2,1,0:T(8,128)} %copy-done.7, f32[2,16,4096]{2,1,0:T(8,128)} %copy-done.36, f32[2,16,4096]{2,1,0:T(8,128)} %copy-done.18, f32[2,16,64]{2,1,0:T(8,128)S(1)} %get-tuple-element.94, f32[2,16,4032]{2,1,0:T(8,128)} %slice.1148, ...), kind=kLoop, calls=%fused_computation.156 | loop fusion | flops 3014656 | bytes 7900928 | tf_op jit(solution)/shard_map/sub | solution.py:48
  240.1 6.7 %collective-permute-start.26 = (f32[2,2,1024]{2,0,1:T(2,128)S(1)}, f32[2,2,1024]{2,0,1:T(2,128)}, u32[]{:S(2)}, u32[]{:S(2)}) collective-permute-start(f32[2,2,1024]{2,0,1:T(2,128)S(1)} %pad_maximum_fusion.29), channel_id=1, source_target_pairs={{0,1},{1,2},{2,3},{3,4},{4,5},{5,6},{6,7},{7,8},{8,9},{9,10},{10,1... | collective-permute-start | bytes 49160 | tf_op jit(solution)/shard_map/ppermute | solution.py:16
  248.5 3.6 %collective-permute-start.27 = (f32[2,2,1,4096]{3,1,2,0:T(2,128)}, f32[2,2,1,4096]{3,1,2,0:T(2,128)S(1)}, u32[]{:S(2)}, u32[]{:S(2)}) collective-permute-start(f32[2,2,1,4096]{3,1,2,0:T(2,128)} %pad_maximum_fusion.13), channel_id=1, source_target_pairs={{0,16},{16,32},{32,48},{48,64},{64,80},{80,96},{96,112},{1,17},{17... | collective-permute-start | bytes 196616 | tf_op jit(solution)/shard_map/ppermute | solution.py:16
  254.3 5.4 %add_reduce_fusion.1 = (f32[16,4096]{1,0:T(8,128)}, f32[16,4096]{1,0:T(8,128)}, f32[2,16,4096]{2,1,0:T(8,128)S(1)}, f32[2,16,4096]{2,1,0:T(8,128)S(1)}, f32[2,16,4096]{2,1,0:T(8,128)S(1)}) fusion(f32[2,16,4096]{2,1,0:T(8,128)} %copy-done.18, f32[2,16,4096]{2,1,0:T(8,128)S(1)} %fusion.191, f32[2,16,4096]{2,1,0:T(8,128)S(1)} %fusion.184, ...), kind=kLoop, calls=%fused_computation.295 | loop fusion | flops 5242880 | bytes 13405952 | tf_op jit(solution)/shard_map/reduce_sum | solution.py:153
  262.5 2.0 slice.1168
  264.5 2.0 slice.1172
  266.5 2.0 slice.1176
  271.4 1.9 collective-permute-start.28
  276.2 2.8 fusion.158
  280.4 6.1 %collective-permute-start.30 = (f32[2,2,1024]{2,0,1:T(2,128)S(1)}, f32[2,2,1024]{2,0,1:T(2,128)S(1)}, u32[]{:S(2)}, u32[]{:S(2)}) collective-permute-start(f32[2,2,1024]{2,0,1:T(2,128)S(1)} %pad_maximum_fusion.31), channel_id=1, source_target_pairs={{0,1},{1,2},{2,3},{3,4},{4,5},{5,6},{6,7},{7,8},{8,9},{9,10},{10,1... | collective-permute-start | bytes 49160 | tf_op jit(solution)/shard_map/ppermute | solution.py:16
  286.6 4.0 %collective-permute-start.31 = (f32[2,2,1,4096]{3,1,2,0:T(2,128)S(1)}, f32[2,2,1,4096]{3,1,2,0:T(2,128)S(1)}, u32[]{:S(2)}, u32[]{:S(2)}) collective-permute-start(f32[2,2,1,4096]{3,1,2,0:T(2,128)S(1)} %pad_maximum_fusion.15), channel_id=1, source_target_pairs={{0,16},{16,32},{32,48},{48,64},{64,80},{80,96},{96,112},{1,17},{17... | collective-permute-start | bytes 196616 | tf_op jit(solution)/shard_map/ppermute | solution.py:16
  292.2 4.2 %fusion.93 = f32[16,4096]{1,0:T(8,128)S(1)} fusion(f32[2,16,4096]{2,1,0:T(8,128)} %copy-done.39, f32[2,16,4096]{2,1,0:T(8,128)} %copy-done.49, f32[2,16,4096]{2,1,0:T(8,128)} %copy-done.31, f32[2,16,4096]{2,1,0:T(8,128)} %copy-done.51, f32[2,16,4096]{2,1,0:T(8,128)} %copy-done.47, f32[2,16,4032]{2,1,0:T(8,128)} %bitcast.413, ...), kind=kLoop, calls=%fused_computation.99 | loop fusion | flops 4128768 | bytes 9998080 | tf_op jit(solution)/shard_map/reduce_sum | solution.py:153
  298.6 1.7 copy.85
  300.3 2.9 reshape.295
  303.2 17.4 %all_to_all.17 = f32[2,1,32768]{2,1,0:T(1,128)S(1)} all-to-all(f32[2,1,32768]{2,1,0:T(1,128)S(1)} %reshape.295), channel_id=1, replica_groups=mesh['src'=2,'gx'=8,'gy'=16] {'src'}, dimensions={0} | all-to-all | bytes 524288 | tf_op jit(solution)/shard_map/all_to_all | solution.py:173
  322.6 2.8 reshape.296
  325.4 2.5 copy.86
  327.9 15.0 %all-to-all-start.1 = ((f32[16,4,2,512]{3,1,2,0:T(4,128)}), f32[16,4,2,512]{3,1,2,0:T(4,128)S(1)}, u32[]{:S(2)}, u32[]{:S(2)}) async-start(f32[16,4,2,512]{3,1,2,0:T(4,128)} %copy.86), calls=%async_computation.1 | async-start | bytes 524288 | tf_op jit(solution)/shard_map/all_to_all | solution.py:172
  342.9 8.7 %all-to-all-done.1 = f32[16,4,2,512]{3,1,2,0:T(4,128)S(1)} async-done(((f32[16,4,2,512]{3,1,2,0:T(4,128)}), f32[16,4,2,512]{3,1,2,0:T(4,128)S(1)}, u32[]{:S(2)}, u32[]{:S(2)}) %all-to-all-start.1) | async-done | bytes 262176 | tf_op jit(solution)/shard_map/all_to_all | solution.py:172
  (419 shorter events, 132.6 us)
Async XLA Ops:
  0.0 14.2 %copy-start.63 = (f32[2,4]{1,0:T(2,128)S(1)}, f32[2,4]{1,0:T(2,128)}, u32[]{:S(2)}) copy-start(f32[2,4]{1,0:T(2,128)} %param.11) | copy-start | bytes 100
  0.0 15.1 %copy-start.68 = (s32[4,16]{1,0:T(4,128)S(1)}, s32[4,16]{1,0:T(4,128)}, u32[]{:S(2)}) copy-start(s32[4,16]{1,0:T(4,128)} %param.13) | copy-start | bytes 772
  0.0 15.1 %copy-start.67 = (s32[4,16]{1,0:T(4,128)S(1)}, s32[4,16]{1,0:T(4,128)}, u32[]{:S(2)}) copy-start(s32[4,16]{1,0:T(4,128)} %param.14) | copy-start | bytes 772
  0.0 15.8 %copy-start.66 = (s32[2,3]{1,0:T(2,128)S(1)}, s32[2,3]{1,0:T(2,128)}, u32[]{:S(2)}) copy-start(s32[2,3]{1,0:T(2,128)} %param.12) | copy-start | bytes 76
  2.3 25.6 %collective-permute-start.3 = (f32[2,2,1,4096]{3,1,2,0:T(2,128)}, f32[2,2,1,4096]{3,1,2,0:T(2,128)}, u32[]{:S(2)}, u32[]{:S(2)}) collective-permute-start(f32[2,2,1,4096]{3,1,2,0:T(2,128)} %pad_maximum_fusion.1), channel_id=1, source_target_pairs={{16,0},{32,16},{48,32},{64,48},{80,64},{96,80},{112,96},{17,1},{33... | collective-permute-start | bytes 196616 | tf_op jit(solution)/shard_map/ppermute | solution.py:16
  4.4 22.1 %collective-permute-start.4 = (f32[2,2,1024]{2,0,1:T(2,128)S(1)}, f32[2,2,1024]{2,0,1:T(2,128)S(1)}, u32[]{:S(2)}, u32[]{:S(2)}) collective-permute-start(f32[2,2,1024]{2,0,1:T(2,128)S(1)} %pad_maximum_fusion.18), channel_id=1, source_target_pairs={{1,0},{2,1},{3,2},{4,3},{5,4},{6,5},{7,6},{8,7},{9,8},{10,9},{11,1... | collective-permute-start | bytes 49160 | tf_op jit(solution)/shard_map/ppermute | solution.py:16
  7.9 23.6 %collective-permute-start = (f32[2,2,1,4096]{3,1,2,0:T(2,128)}, f32[2,2,1,4096]{3,1,2,0:T(2,128)}, u32[]{:S(2)}, u32[]{:S(2)}) collective-permute-start(f32[2,2,1,4096]{3,1,2,0:T(2,128)} %pad_maximum_fusion), channel_id=1, source_target_pairs={{16,0},{32,16},{48,32},{64,48},{80,64},{96,80},{112,96},{17,1},{33... | collective-permute-start | bytes 196616 | tf_op jit(solution)/shard_map/ppermute | solution.py:16
  11.9 15.3 %collective-permute-start.1 = (f32[2,2,1024]{2,0,1:T(2,128)S(1)}, f32[2,2,1024]{2,0,1:T(2,128)S(1)}, u32[]{:S(2)}, u32[]{:S(2)}) collective-permute-start(f32[2,2,1024]{2,0,1:T(2,128)S(1)} %pad_maximum_fusion.16), channel_id=1, source_target_pairs={{1,0},{2,1},{3,2},{4,3},{5,4},{6,5},{7,6},{8,7},{9,8},{10,9},{11,1... | collective-permute-start | bytes 49160 | tf_op jit(solution)/shard_map/ppermute | solution.py:16
  15.9 72.1 %copy-start.64 = (s32[2]{0:T(128)}, s32[2]{0:T(128)S(1)}, u32[]{:S(2)}) copy-start(s32[2]{0:T(128)S(1)} %get-tuple-element.12) | copy-start | bytes 28
  25.5 7.0 %copy-start.56 = (f32[2,15,4096]{2,1,0:T(8,128)S(1)}, f32[2,15,4096]{2,1,0:T(8,128)}, u32[]{:S(2)}) copy-start(f32[2,15,4096]{2,1,0:T(8,128)} %slice.972) | copy-start | bytes 1474564
  26.5 6.0 %copy-start.57 = (f32[2,16,4032]{2,1,0:T(8,128)S(1)}, f32[2,16,4032]{2,1,0:T(8,128)}, u32[]{:S(2)}) copy-start(f32[2,16,4032]{2,1,0:T(8,128)} %slice.976) | copy-start | bytes 1548292
  28.9 6.0 %copy-start = (f32[2,6,16,4096]{3,2,1,0:T(8,128)S(1)}, f32[2,6,16,4096]{3,2,1,0:T(8,128)}, u32[]{:S(2)}) copy-start(f32[2,6,16,4096]{3,2,1,0:T(8,128)} %param.8) | copy-start | bytes 9437188
  28.9 6.0 %copy-start.52 = (f32[2,15,4096]{2,1,0:T(8,128)S(1)}, f32[2,15,4096]{2,1,0:T(8,128)}, u32[]{:S(2)}) copy-start(f32[2,15,4096]{2,1,0:T(8,128)} %slice.1007) | copy-start | bytes 1474564
  30.8 28.9 %copy-start.22 = (f32[2,16,4096]{2,1,0:T(8,128)}, f32[2,16,4096]{2,1,0:T(8,128)S(1)}, u32[]{:S(2)}) copy-start(f32[2,16,4096]{2,1,0:T(8,128)S(1)} %fusion.173) | copy-start | bytes 1572868
  34.0 13.6 %copy-start.13 = (f32[2,16,4096]{2,1,0:T(8,128)}, f32[2,16,4096]{2,1,0:T(8,128)S(1)}, u32[]{:S(2)}) copy-start(f32[2,16,4096]{2,1,0:T(8,128)S(1)} %fusion.170) | copy-start | bytes 1572868
  36.8 18.3 %collective-permute-start.5 = (f32[2,2,1024]{2,0,1:T(2,128)}, f32[2,2,1024]{2,0,1:T(2,128)}, u32[]{:S(2)}, u32[]{:S(2)}) collective-permute-start(f32[2,2,1024]{2,0,1:T(2,128)} %pad_maximum_fusion.19), channel_id=1, source_target_pairs={{0,1},{1,2},{2,3},{3,4},{4,5},{5,6},{6,7},{7,8},{8,9},{9,10},{10,1... | collective-permute-start | bytes 49160 | tf_op jit(solution)/shard_map/ppermute | solution.py:16
  43.0 14.2 %collective-permute-start.6 = (f32[2,2,1,4096]{3,1,2,0:T(2,128)}, f32[2,2,1,4096]{3,1,2,0:T(2,128)}, u32[]{:S(2)}, u32[]{:S(2)}) collective-permute-start(f32[2,2,1,4096]{3,1,2,0:T(2,128)} %pad_maximum_fusion.2), channel_id=1, source_target_pairs={{0,16},{16,32},{32,48},{48,64},{64,80},{80,96},{96,112},{1,17},{17... | collective-permute-start | bytes 196616 | tf_op jit(solution)/shard_map/ppermute | solution.py:16
  45.0 13.3 %copy-start.71 = (f32[2]{0:T(128)S(1)}, f32[2]{0:T(128)}, u32[]{:S(2)}) copy-start(f32[2]{0:T(128)} %get-tuple-element.9) | copy-start | bytes 28
  47.7 12.0 %copy-start.29 = (f32[2,16,4096]{2,1,0:T(8,128)}, f32[2,16,4096]{2,1,0:T(8,128)S(1)}, u32[]{:S(2)}) copy-start(f32[2,16,4096]{2,1,0:T(8,128)S(1)} %get-tuple-element.23) | copy-start | bytes 1572868
  47.7 12.0 %copy-start.37 = (f32[2,16,4096]{2,1,0:T(8,128)}, f32[2,16,4096]{2,1,0:T(8,128)S(1)}, u32[]{:S(2)}) copy-start(f32[2,16,4096]{2,1,0:T(8,128)S(1)} %get-tuple-element.22) | copy-start | bytes 1572868
  48.5 14.3 %collective-permute-start.18 = (f32[2,2,1,4096]{3,1,2,0:T(2,128)}, f32[2,2,1,4096]{3,1,2,0:T(2,128)}, u32[]{:S(2)}, u32[]{:S(2)}) collective-permute-start(f32[2,2,1,4096]{3,1,2,0:T(2,128)} %pad_maximum_fusion.8), channel_id=1, source_target_pairs={{0,16},{16,32},{32,48},{48,64},{64,80},{80,96},{96,112},{1,17},{17... | collective-permute-start | bytes 196616 | tf_op jit(solution)/shard_map/ppermute | solution.py:16
  51.8 4.8 %collective-permute-start.2 = (f32[2,2,1024]{2,0,1:T(2,128)S(1)}, f32[2,2,1024]{2,0,1:T(2,128)S(1)}, u32[]{:S(2)}, u32[]{:S(2)}) collective-permute-start(f32[2,2,1024]{2,0,1:T(2,128)S(1)} %pad_maximum_fusion.17), channel_id=1, source_target_pairs={{0,1},{1,2},{2,3},{3,4},{4,5},{5,6},{6,7},{7,8},{8,9},{9,10},{10,1... | collective-permute-start | bytes 49160 | tf_op jit(solution)/shard_map/ppermute | solution.py:16
  61.6 10.5 %collective-permute-start.8 = (f32[2,2,1024]{2,0,1:T(2,128)S(1)}, f32[2,2,1024]{2,0,1:T(2,128)S(1)}, u32[]{:S(2)}, u32[]{:S(2)}) collective-permute-start(f32[2,2,1024]{2,0,1:T(2,128)S(1)} %pad_maximum_fusion.20), channel_id=1, source_target_pairs={{1,0},{2,1},{3,2},{4,3},{5,4},{6,5},{7,6},{8,7},{9,8},{10,9},{11,1... | collective-permute-start | bytes 49160 | tf_op jit(solution)/shard_map/ppermute | solution.py:16
  69.6 4.3 %collective-permute-start.7 = (f32[2,2,1,4096]{3,1,2,0:T(2,128)S(1)}, f32[2,2,1,4096]{3,1,2,0:T(2,128)S(1)}, u32[]{:S(2)}, u32[]{:S(2)}) collective-permute-start(f32[2,2,1,4096]{3,1,2,0:T(2,128)S(1)} %pad_maximum_fusion.3), channel_id=1, source_target_pairs={{16,0},{32,16},{48,32},{64,48},{80,64},{96,80},{112,96},{17,1},{33... | collective-permute-start | bytes 196616 | tf_op jit(solution)/shard_map/ppermute | solution.py:16
  74.0 14.1 %copy-start.70 = (f32[2]{0:T(128)S(1)}, f32[2]{0:T(128)}, u32[]{:S(2)}) copy-start(f32[2]{0:T(128)} %get-tuple-element.8) | copy-start | bytes 28
  77.7 8.1 %collective-permute-start.9 = (f32[2,2,1024]{2,0,1:T(2,128)S(1)}, f32[2,2,1024]{2,0,1:T(2,128)S(1)}, u32[]{:S(2)}, u32[]{:S(2)}) collective-permute-start(f32[2,2,1024]{2,0,1:T(2,128)S(1)} %pad_maximum_fusion.21), channel_id=1, source_target_pairs={{0,1},{1,2},{2,3},{3,4},{4,5},{5,6},{6,7},{7,8},{8,9},{9,10},{10,1... | collective-permute-start | bytes 49160 | tf_op jit(solution)/shard_map/ppermute | solution.py:16
  82.4 5.6 %collective-permute-start.10 = (f32[2,2,1,4096]{3,1,2,0:T(2,128)S(1)}, f32[2,2,1,4096]{3,1,2,0:T(2,128)S(1)}, u32[]{:S(2)}, u32[]{:S(2)}) collective-permute-start(f32[2,2,1,4096]{3,1,2,0:T(2,128)S(1)} %pad_maximum_fusion.4), channel_id=1, source_target_pairs={{0,16},{16,32},{32,48},{48,64},{64,80},{80,96},{96,112},{1,17},{17... | collective-permute-start | bytes 196616 | tf_op jit(solution)/shard_map/ppermute | solution.py:16
  91.5 18.6 %copy-start.1 = (f32[2,16,4096]{2,1,0:T(8,128)}, f32[2,16,4096]{2,1,0:T(8,128)S(1)}, u32[]{:S(2)}) copy-start(f32[2,16,4096]{2,1,0:T(8,128)S(1)} %get-tuple-element.36) | copy-start | bytes 1572868
  95.7 6.3 %copy-start.6 = (f32[2,16,4096]{2,1,0:T(8,128)S(1)}, f32[2,16,4096]{2,1,0:T(8,128)}, u32[]{:S(2)}) copy-start(f32[2,16,4096]{2,1,0:T(8,128)} %get-tuple-element.37) | copy-start | bytes 1572868
  96.4 10.4 %collective-permute-start.12 = (f32[2,2,1024]{2,0,1:T(2,128)S(1)}, f32[2,2,1024]{2,0,1:T(2,128)}, u32[]{:S(2)}, u32[]{:S(2)}) collective-permute-start(f32[2,2,1024]{2,0,1:T(2,128)S(1)} %pad_maximum_fusion.22), channel_id=1, source_target_pairs={{1,0},{2,1},{3,2},{4,3},{5,4},{6,5},{7,6},{8,7},{9,8},{10,9},{11,1... | collective-permute-start | bytes 49160 | tf_op jit(solution)/shard_map/ppermute | solution.py:16
  105.0 4.1 %collective-permute-start.11 = (f32[2,2,1,4096]{3,1,2,0:T(2,128)}, f32[2,2,1,4096]{3,1,2,0:T(2,128)}, u32[]{:S(2)}, u32[]{:S(2)}) collective-permute-start(f32[2,2,1,4096]{3,1,2,0:T(2,128)} %pad_maximum_fusion.5), channel_id=1, source_target_pairs={{16,0},{32,16},{48,32},{64,48},{80,64},{96,80},{112,96},{17,1},{33... | collective-permute-start | bytes 196616 | tf_op jit(solution)/shard_map/ppermute | solution.py:16
  110.1 16.7 %copy-start.65 = (s32[2]{0:T(128)S(1)}, s32[2]{0:T(128)}, u32[]{:S(2)}) copy-start(s32[2]{0:T(128)} %copy-done.64) | copy-start | bytes 28
  110.1 16.7 %copy-start.69 = (f32[2]{0:T(128)S(1)}, f32[2]{0:T(128)}, u32[]{:S(2)}) copy-start(f32[2]{0:T(128)} %get-tuple-element.10) | copy-start | bytes 28
  114.9 9.9 %collective-permute-start.13 = (f32[2,2,1024]{2,0,1:T(2,128)S(1)}, f32[2,2,1024]{2,0,1:T(2,128)S(1)}, u32[]{:S(2)}, u32[]{:S(2)}) collective-permute-start(f32[2,2,1024]{2,0,1:T(2,128)S(1)} %pad_maximum_fusion.23), channel_id=1, source_target_pairs={{0,1},{1,2},{2,3},{3,4},{4,5},{5,6},{6,7},{7,8},{8,9},{9,10},{10,1... | collective-permute-start | bytes 49160 | tf_op jit(solution)/shard_map/ppermute | solution.py:16
  121.1 5.6 %collective-permute-start.14 = (f32[2,2,1,4096]{3,1,2,0:T(2,128)S(1)}, f32[2,2,1,4096]{3,1,2,0:T(2,128)S(1)}, u32[]{:S(2)}, u32[]{:S(2)}) collective-permute-start(f32[2,2,1,4096]{3,1,2,0:T(2,128)S(1)} %pad_maximum_fusion.6), channel_id=1, source_target_pairs={{0,16},{16,32},{32,48},{48,64},{64,80},{80,96},{96,112},{1,17},{17... | collective-permute-start | bytes 196616 | tf_op jit(solution)/shard_map/ppermute | solution.py:16
  135.7 6.4 %copy-start.5 = (f32[2,16,4096]{2,1,0:T(8,128)S(1)}, f32[2,16,4096]{2,1,0:T(8,128)}, u32[]{:S(2)}) copy-start(f32[2,16,4096]{2,1,0:T(8,128)} %get-tuple-element.35) | copy-start | bytes 1572868
  136.5 10.6 %collective-permute-start.16 = (f32[2,2,1024]{2,0,1:T(2,128)S(1)}, f32[2,2,1024]{2,0,1:T(2,128)}, u32[]{:S(2)}, u32[]{:S(2)}) collective-permute-start(f32[2,2,1024]{2,0,1:T(2,128)S(1)} %pad_maximum_fusion.24), channel_id=1, source_target_pairs={{1,0},{2,1},{3,2},{4,3},{5,4},{6,5},{7,6},{8,7},{9,8},{10,9},{11,1... | collective-permute-start | bytes 49160 | tf_op jit(solution)/shard_map/ppermute | solution.py:16
  145.2 4.1 %collective-permute-start.15 = (f32[2,2,1,4096]{3,1,2,0:T(2,128)}, f32[2,2,1,4096]{3,1,2,0:T(2,128)}, u32[]{:S(2)}, u32[]{:S(2)}) collective-permute-start(f32[2,2,1,4096]{3,1,2,0:T(2,128)} %pad_maximum_fusion.7), channel_id=1, source_target_pairs={{16,0},{32,16},{48,32},{64,48},{80,64},{96,80},{112,96},{17,1},{33... | collective-permute-start | bytes 196616 | tf_op jit(solution)/shard_map/ppermute | solution.py:16
  158.9 10.6 %collective-permute-start.17 = (f32[2,2,1024]{2,0,1:T(2,128)S(1)}, f32[2,2,1024]{2,0,1:T(2,128)}, u32[]{:S(2)}, u32[]{:S(2)}) collective-permute-start(f32[2,2,1024]{2,0,1:T(2,128)S(1)} %pad_maximum_fusion.25), channel_id=1, source_target_pairs={{0,1},{1,2},{2,3},{3,4},{4,5},{5,6},{6,7},{7,8},{8,9},{9,10},{10,1... | collective-permute-start | bytes 49160 | tf_op jit(solution)/shard_map/ppermute | solution.py:16
  165.8 5.9 %collective-permute-start.19 = (f32[2,2,1,4096]{3,1,2,0:T(2,128)}, f32[2,2,1,4096]{3,1,2,0:T(2,128)}, u32[]{:S(2)}, u32[]{:S(2)}) collective-permute-start(f32[2,2,1,4096]{3,1,2,0:T(2,128)} %pad_maximum_fusion.9), channel_id=1, source_target_pairs={{0,16},{16,32},{32,48},{48,64},{64,80},{80,96},{96,112},{1,17},{17... | collective-permute-start | bytes 196616 | tf_op jit(solution)/shard_map/ppermute | solution.py:16
  180.4 8.1 %copy-start.34 = (f32[2,16,4096]{2,1,0:T(8,128)S(1)}, f32[2,16,4096]{2,1,0:T(8,128)}, u32[]{:S(2)}) copy-start(f32[2,16,4096]{2,1,0:T(8,128)} %copy-done.33) | copy-start | bytes 1572868
  180.4 9.1 %copy-start.42 = (f32[2,16,4096]{2,1,0:T(8,128)S(1)}, f32[2,16,4096]{2,1,0:T(8,128)}, u32[]{:S(2)}) copy-start(f32[2,16,4096]{2,1,0:T(8,128)} %copy-done.41) | copy-start | bytes 1572868
  180.4 10.2 %copy-start.21 = (f32[2,16,4096]{2,1,0:T(8,128)S(1)}, f32[2,16,4096]{2,1,0:T(8,128)}, u32[]{:S(2)}) copy-start(f32[2,16,4096]{2,1,0:T(8,128)} %copy-done.20) | copy-start | bytes 1572868
  180.4 12.9 %collective-permute-start.21 = (f32[2,2,1024]{2,0,1:T(2,128)S(1)}, f32[2,2,1024]{2,0,1:T(2,128)}, u32[]{:S(2)}, u32[]{:S(2)}) collective-permute-start(f32[2,2,1024]{2,0,1:T(2,128)S(1)} %pad_maximum_fusion.26), channel_id=1, source_target_pairs={{1,0},{2,1},{3,2},{4,3},{5,4},{6,5},{7,6},{8,7},{9,8},{10,9},{11,1... | collective-permute-start | bytes 49160 | tf_op jit(solution)/shard_map/ppermute | solution.py:16
  191.4 4.1 %collective-permute-start.20 = (f32[2,2,1,4096]{3,1,2,0:T(2,128)}, f32[2,2,1,4096]{3,1,2,0:T(2,128)S(1)}, u32[]{:S(2)}, u32[]{:S(2)}) collective-permute-start(f32[2,2,1,4096]{3,1,2,0:T(2,128)} %pad_maximum_fusion.10), channel_id=1, source_target_pairs={{16,0},{32,16},{48,32},{64,48},{80,64},{96,80},{112,96},{17,1},{33... | collective-permute-start | bytes 196616 | tf_op jit(solution)/shard_map/ppermute | solution.py:16
  200.9 11.9 %collective-permute-start.22 = (f32[2,2,1024]{2,0,1:T(2,128)S(1)}, f32[2,2,1024]{2,0,1:T(2,128)}, u32[]{:S(2)}, u32[]{:S(2)}) collective-permute-start(f32[2,2,1024]{2,0,1:T(2,128)S(1)} %pad_maximum_fusion.27), channel_id=1, source_target_pairs={{0,1},{1,2},{2,3},{3,4},{4,5},{5,6},{6,7},{7,8},{8,9},{9,10},{10,1... | collective-permute-start | bytes 49160 | tf_op jit(solution)/shard_map/ppermute | solution.py:16
  209.3 5.8 %collective-permute-start.23 = (f32[2,2,1,4096]{3,1,2,0:T(2,128)}, f32[2,2,1,4096]{3,1,2,0:T(2,128)S(1)}, u32[]{:S(2)}, u32[]{:S(2)}) collective-permute-start(f32[2,2,1,4096]{3,1,2,0:T(2,128)} %pad_maximum_fusion.11), channel_id=1, source_target_pairs={{0,16},{16,32},{32,48},{48,64},{64,80},{80,96},{96,112},{1,17},{17... | collective-permute-start | bytes 196616 | tf_op jit(solution)/shard_map/ppermute | solution.py:16
  219.5 8.1 %copy-start.45 = (f32[2,16,4096]{2,1,0:T(8,128)S(1)}, f32[2,16,4096]{2,1,0:T(8,128)}, u32[]{:S(2)}) copy-start(f32[2,16,4096]{2,1,0:T(8,128)} %copy-done.44) | copy-start | bytes 1572868
  219.5 9.2 %copy-start.19 = (f32[2,16,4096]{2,1,0:T(8,128)S(1)}, f32[2,16,4096]{2,1,0:T(8,128)}, u32[]{:S(2)}) copy-start(f32[2,16,4096]{2,1,0:T(8,128)} %copy-done.18) | copy-start | bytes 1572868
  219.6 13.0 %collective-permute-start.25 = (f32[2,2,1024]{2,0,1:T(2,128)S(1)}, f32[2,2,1024]{2,0,1:T(2,128)}, u32[]{:S(2)}, u32[]{:S(2)}) collective-permute-start(f32[2,2,1024]{2,0,1:T(2,128)S(1)} %pad_maximum_fusion.28), channel_id=1, source_target_pairs={{1,0},{2,1},{3,2},{4,3},{5,4},{6,5},{7,6},{8,7},{9,8},{10,9},{11,1... | collective-permute-start | bytes 49160 | tf_op jit(solution)/shard_map/ppermute | solution.py:16
  230.6 4.1 %collective-permute-start.24 = (f32[2,2,1,4096]{3,1,2,0:T(2,128)}, f32[2,2,1,4096]{3,1,2,0:T(2,128)S(1)}, u32[]{:S(2)}, u32[]{:S(2)}) collective-permute-start(f32[2,2,1,4096]{3,1,2,0:T(2,128)} %pad_maximum_fusion.12), channel_id=1, source_target_pairs={{16,0},{32,16},{48,32},{64,48},{80,64},{96,80},{112,96},{17,1},{33... | collective-permute-start | bytes 196616 | tf_op jit(solution)/shard_map/ppermute | solution.py:16
  240.1 11.9 %collective-permute-start.26 = (f32[2,2,1024]{2,0,1:T(2,128)S(1)}, f32[2,2,1024]{2,0,1:T(2,128)}, u32[]{:S(2)}, u32[]{:S(2)}) collective-permute-start(f32[2,2,1024]{2,0,1:T(2,128)S(1)} %pad_maximum_fusion.29), channel_id=1, source_target_pairs={{0,1},{1,2},{2,3},{3,4},{4,5},{5,6},{6,7},{7,8},{8,9},{9,10},{10,1... | collective-permute-start | bytes 49160 | tf_op jit(solution)/shard_map/ppermute | solution.py:16
  248.5 5.8 %collective-permute-start.27 = (f32[2,2,1,4096]{3,1,2,0:T(2,128)}, f32[2,2,1,4096]{3,1,2,0:T(2,128)S(1)}, u32[]{:S(2)}, u32[]{:S(2)}) collective-permute-start(f32[2,2,1,4096]{3,1,2,0:T(2,128)} %pad_maximum_fusion.13), channel_id=1, source_target_pairs={{0,16},{16,32},{32,48},{48,64},{64,80},{80,96},{96,112},{1,17},{17... | collective-permute-start | bytes 196616 | tf_op jit(solution)/shard_map/ppermute | solution.py:16
  260.5 10.1 %copy-start.17 = (f32[2,16,4096]{2,1,0:T(8,128)S(1)}, f32[2,16,4096]{2,1,0:T(8,128)}, u32[]{:S(2)}) copy-start(f32[2,16,4096]{2,1,0:T(8,128)} %copy-done.16) | copy-start | bytes 1572868
  261.0 7.6 %copy-start.32 = (f32[2,16,4096]{2,1,0:T(8,128)S(1)}, f32[2,16,4096]{2,1,0:T(8,128)}, u32[]{:S(2)}) copy-start(f32[2,16,4096]{2,1,0:T(8,128)} %copy-done.31) | copy-start | bytes 1572868
  261.0 8.6 %copy-start.40 = (f32[2,16,4096]{2,1,0:T(8,128)S(1)}, f32[2,16,4096]{2,1,0:T(8,128)}, u32[]{:S(2)}) copy-start(f32[2,16,4096]{2,1,0:T(8,128)} %copy-done.39) | copy-start | bytes 1572868
  261.0 12.3 %collective-permute-start.29 = (f32[2,2,1024]{2,0,1:T(2,128)S(1)}, f32[2,2,1024]{2,0,1:T(2,128)}, u32[]{:S(2)}, u32[]{:S(2)}) collective-permute-start(f32[2,2,1024]{2,0,1:T(2,128)S(1)} %pad_maximum_fusion.30), channel_id=1, source_target_pairs={{1,0},{2,1},{3,2},{4,3},{5,4},{6,5},{7,6},{8,7},{9,8},{10,9},{11,1... | collective-permute-start | bytes 49160 | tf_op jit(solution)/shard_map/ppermute | solution.py:16
  262.5 13.7 %copy-start.15 = (f32[2,16,4096]{2,1,0:T(8,128)S(1)}, f32[2,16,4096]{2,1,0:T(8,128)}, u32[]{:S(2)}) copy-start(f32[2,16,4096]{2,1,0:T(8,128)} %copy-done.14) | copy-start | bytes 1572868
  262.5 13.7 %copy-start.30 = (f32[2,16,4096]{2,1,0:T(8,128)S(1)}, f32[2,16,4096]{2,1,0:T(8,128)}, u32[]{:S(2)}) copy-start(f32[2,16,4096]{2,1,0:T(8,128)} %get-tuple-element.42) | copy-start | bytes 1572868
  271.4 3.8 %collective-permute-start.28 = (f32[2,2,1,4096]{3,1,2,0:T(2,128)S(1)}, f32[2,2,1,4096]{3,1,2,0:T(2,128)}, u32[]{:S(2)}, u32[]{:S(2)}) collective-permute-start(f32[2,2,1,4096]{3,1,2,0:T(2,128)S(1)} %pad_maximum_fusion.14), channel_id=1, source_target_pairs={{16,0},{32,16},{48,32},{64,48},{80,64},{96,80},{112,96},{17,1},{33... | collective-permute-start | bytes 196616 | tf_op jit(solution)/shard_map/ppermute | solution.py:16
  280.4 10.2 %collective-permute-start.30 = (f32[2,2,1024]{2,0,1:T(2,128)S(1)}, f32[2,2,1024]{2,0,1:T(2,128)S(1)}, u32[]{:S(2)}, u32[]{:S(2)}) collective-permute-start(f32[2,2,1024]{2,0,1:T(2,128)S(1)} %pad_maximum_fusion.31), channel_id=1, source_target_pairs={{0,1},{1,2},{2,3},{3,4},{4,5},{5,6},{6,7},{7,8},{8,9},{9,10},{10,1... | collective-permute-start | bytes 49160 | tf_op jit(solution)/shard_map/ppermute | solution.py:16
  286.6 5.6 %collective-permute-start.31 = (f32[2,2,1,4096]{3,1,2,0:T(2,128)S(1)}, f32[2,2,1,4096]{3,1,2,0:T(2,128)S(1)}, u32[]{:S(2)}, u32[]{:S(2)}) collective-permute-start(f32[2,2,1,4096]{3,1,2,0:T(2,128)S(1)} %pad_maximum_fusion.15), channel_id=1, source_target_pairs={{0,16},{16,32},{32,48},{48,64},{64,80},{80,96},{96,112},{1,17},{17... | collective-permute-start | bytes 196616 | tf_op jit(solution)/shard_map/ppermute | solution.py:16
  303.2 39.7 %copy-start.72 = (s32[1,64]{1,0:T(1,128)S(1)}, s32[1,64]{1,0:T(1,128)}, u32[]{:S(2)}) copy-start(s32[1,64]{1,0:T(1,128)} %param.15) | copy-start | bytes 772
  327.9 23.7 %all-to-all-start.1 = ((f32[16,4,2,512]{3,1,2,0:T(4,128)}), f32[16,4,2,512]{3,1,2,0:T(4,128)S(1)}, u32[]{:S(2)}, u32[]{:S(2)}) async-start(f32[16,4,2,512]{3,1,2,0:T(4,128)} %copy.86), calls=%async_computation.1 | async-start | bytes 524288 | tf_op jit(solution)/shard_map/all_to_all | solution.py:172
  (42 other events, 110.0 us)
where the time goes:
time: 357 us; the launch traced here: 353 us
  local copies, waits for them, and re-layouts  122 us (34%)
  starting transfers between devices  113 us (32%)
  other arithmetic  71.6 us (20%)
  waiting for transfers between devices  26.9 us (8%)
  blocking collectives  17.4 us (5%)
    ppermute x32, starting transfers between devices, passed_along(): return lax.ppermute(shard, axis, pairs)  98.2 us
    sub x8, other arithmetic, magnetic_update(): magnetic[0]  23.2 us
    slice x16, local copies, waits for them, and re-layouts, upper_y(): return jnp.concatenate([values[..., z_cells:], ghosts], axis=-1)  21.3 us
    ppermute x32, waiting for transfers between devices, passed_along(): return lax.ppermute(shard, axis, pairs)  18.3 us
    all_to_all x1, blocking collectives, per_device(): lax.all_to_all(sectioned, 'src', split_axis=3, concat_axis=2, tiled=True)  17.4 us
    slice x16, local copies, waits for them, and re-layouts, upper_z(): values[..., 1:]  17.2 us
    reduce_sum x3, other arithmetic, per_device(): density = density + jnp.sum(intersection, axis=0)  16 us
    slice x16, local copies, waits for them, and re-layouts, upper_x(): return jnp.concatenate([values[..., 1:, :], ghosts], axis=-2)  15.9 us
  transfers between devices with their start and end apart: 33, of which 14 were waited for; matrix products, arithmetic and copies ran while one was open for 27% of the time, Pallas kernels for 0%

commit v1 on v0

--- a/solution.py
+++ b/solution.py
@@ -170,7 +170,12 @@
     )
     sectioned = outgoing.reshape(peers, capacity, 1, -1)
     arrived = lax.all_to_all(
-        lax.all_to_all(sectioned, "src", split_axis=3, concat_axis=2, tiled=True),
+        jnp.concatenate(
+            lax.all_to_all(
+                jnp.stack(jnp.split(sectioned, lax.axis_size("src"), axis=3)), "src", 0, 0
+            ),
+            axis=2,
+        ),
         "gy",
         split_axis=0,
         concat_axis=0,

time: 357 us -> 353 us (0.989)
    unnamed x148 -> x178, local copies, waits for them, and re-layouts: 15 us -> 11.8 us
where the time goes in v1:
time: 353 us; the launch traced here: 349 us
  local copies, waits for them, and re-layouts  120 us (34%)
  starting transfers between devices  113 us (32%)
  other arithmetic  69.5 us (20%)
  waiting for transfers between devices  27.6 us (8%)
  blocking collectives  17.4 us (5%)
    ppermute x32, starting transfers between devices, passed_along(): return lax.ppermute(shard, axis, pairs)  98.2 us
    sub x8, other arithmetic, magnetic_update(): magnetic[0]  24.1 us
    slice x16, local copies, waits for them, and re-layouts, upper_y(): return jnp.concatenate([values[..., z_cells:], ghosts], axis=-1)  22.5 us
    ppermute x32, waiting for transfers between devices, passed_along(): return lax.ppermute(shard, axis, pairs)  19 us
    slice x16, local copies, waits for them, and re-layouts, upper_z(): values[..., 1:]  18.3 us
    slice x16, local copies, waits for them, and re-layouts, upper_x(): return jnp.concatenate([values[..., 1:, :], ghosts], axis=-2)  17.9 us
    all_to_all x1, blocking collectives, per_device(): lax.all_to_all(jnp.stack(jnp.split(sectioned, lax.axis_size('src'), axis=...  17.4 us
    reduce_sum x3, other arithmetic, per_device(): density = density + jnp.sum(intersection, axis=0)  16.5 us
  transfers between devices with their start and end apart: 33, of which 14 were waited for; matrix products, arithmetic and copies ran while one was open for 27% of the time, Pallas kernels for 0%

profile of v1, /device:TPU:32, one launch (start us, length us, event | category | flops | bytes accessed | tf_op | source)
XLA Modules:
  0.0 349.3 jit_solution(14620851322780358808)
XLA Ops:
  0.0 2.4 slice_bitcast_fusion.2
  4.0 1.9 collective-permute-start.3
  10.6 3.8 %collective-permute-start = (f32[2,2,1,4096]{3,1,2,0:T(2,128)}, f32[2,2,1,4096]{3,1,2,0:T(2,128)}, u32[]{:S(2)}, u32[]{:S(2)}) collective-permute-start(f32[2,2,1,4096]{3,1,2,0:T(2,128)} %pad_maximum_fusion.1), channel_id=1, source_target_pairs={{16,0},{32,16},{48,32},{64,48},{80,64},{96,80},{112,96},{17,1},{33... | collective-permute-start | bytes 196616 | tf_op jit(solution)/shard_map/ppermute | solution.py:16
  18.3 1.9 slice.1007
  20.3 2.0 slice.999
  23.3 2.1 slice.1006
  35.5 2.0 fusion.173
  39.3 1.6 fusion.170
  44.7 4.9 %collective-permute-start.5 = (f32[2,2,1024]{2,0,1:T(2,128)S(1)}, f32[2,2,1024]{2,0,1:T(2,128)S(1)}, u32[]{:S(2)}, u32[]{:S(2)}) collective-permute-start(f32[2,2,1024]{2,0,1:T(2,128)S(1)} %pad_maximum_fusion.20), channel_id=1, source_target_pairs={{0,1},{1,2},{2,3},{3,4},{4,5},{5,6},{6,7},{7,8},{8,9},{9,10},{10,1... | collective-permute-start | bytes 49160 | tf_op jit(solution)/shard_map/ppermute | solution.py:16
  50.6 1.9 collective-permute-start.6
  52.6 2.8 fusion.102
  56.1 2.3 collective-permute-start.18
  58.7 3.9 %collective-permute-start.2 = (f32[2,2,1024]{2,0,1:T(2,128)S(1)}, f32[2,2,1024]{2,0,1:T(2,128)S(1)}, u32[]{:S(2)}, u32[]{:S(2)}) collective-permute-start(f32[2,2,1024]{2,0,1:T(2,128)S(1)} %pad_maximum_fusion.18), channel_id=1, source_target_pairs={{0,1},{1,2},{2,3},{3,4},{4,5},{5,6},{6,7},{7,8},{8,9},{9,10},{10,1... | collective-permute-start | bytes 49160 | tf_op jit(solution)/shard_map/ppermute | solution.py:16
  66.2 1.7 fusion.43
  76.2 2.4 collective-permute-start.7
  78.7 1.8 collective-permute-done.7
  80.6 2.5 fusion.118
  84.3 4.5 %collective-permute-start.9 = (f32[2,2,1024]{2,0,1:T(2,128)S(1)}, f32[2,2,1024]{2,0,1:T(2,128)S(1)}, u32[]{:S(2)}, u32[]{:S(2)}) collective-permute-start(f32[2,2,1024]{2,0,1:T(2,128)S(1)} %pad_maximum_fusion.22), channel_id=1, source_target_pairs={{0,1},{1,2},{2,3},{3,4},{4,5},{5,6},{6,7},{7,8},{8,9},{9,10},{10,1... | collective-permute-start | bytes 49160 | tf_op jit(solution)/shard_map/ppermute | solution.py:16
  88.9 3.5 %collective-permute-start.10 = (f32[2,2,1,4096]{3,1,2,0:T(2,128)S(1)}, f32[2,2,1,4096]{3,1,2,0:T(2,128)S(1)}, u32[]{:S(2)}, u32[]{:S(2)}) collective-permute-start(f32[2,2,1,4096]{3,1,2,0:T(2,128)S(1)} %pad_maximum_fusion.5), channel_id=1, source_target_pairs={{0,16},{16,32},{32,48},{48,64},{64,80},{80,96},{96,112},{1,17},{17... | collective-permute-start | bytes 196616 | tf_op jit(solution)/shard_map/ppermute | solution.py:16
  92.5 2.0 collective-permute-done.10
  94.6 1.5 fusion.184
  104.3 1.5 pad_maximum_fusion.6
  111.5 1.9 collective-permute-start.11
  116.6 3.7 %fusion.126 = (f32[2,16,4096]{2,1,0:T(8,128)S(1)}, f32[2,16,4096]{2,1,0:T(8,128)}, f32[2,16,4096]{2,1,0:T(8,128)S(1)}) fusion(f32[2,16,4096]{2,1,0:T(8,128)} %copy-done.12, f32[2,16,4096]{2,1,0:T(8,128)S(1)} %get-tuple-element.36, f32[2,16,4096]{2,1,0:T(8,128)S(1)} %fusion.184, f32[2,16,64]{2,1,0:T(8,128)S(1)} %get-tuple-element.112, ...), kind=kLoop, calls=%fused_computation.132 | loop fusion | flops 3014656 | bytes 7900928 | tf_op jit(solution)/shard_map/sub | solution.py:48
  121.5 5.1 %collective-permute-start.13 = (f32[2,2,1024]{2,0,1:T(2,128)S(1)}, f32[2,2,1024]{2,0,1:T(2,128)S(1)}, u32[]{:S(2)}, u32[]{:S(2)}) collective-permute-start(f32[2,2,1024]{2,0,1:T(2,128)S(1)} %pad_maximum_fusion.24), channel_id=1, source_target_pairs={{0,1},{1,2},{2,3},{3,4},{4,5},{5,6},{6,7},{7,8},{8,9},{9,10},{10,1... | collective-permute-start | bytes 49160 | tf_op jit(solution)/shard_map/ppermute | solution.py:16
  127.7 3.7 %collective-permute-start.14 = (f32[2,2,1,4096]{3,1,2,0:T(2,128)S(1)}, f32[2,2,1,4096]{3,1,2,0:T(2,128)S(1)}, u32[]{:S(2)}, u32[]{:S(2)}) collective-permute-start(f32[2,2,1,4096]{3,1,2,0:T(2,128)S(1)} %pad_maximum_fusion.7), channel_id=1, source_target_pairs={{0,16},{16,32},{32,48},{48,64},{64,80},{80,96},{96,112},{1,17},{17... | collective-permute-start | bytes 196616 | tf_op jit(solution)/shard_map/ppermute | solution.py:16
  131.5 1.8 collective-permute-done.14
  133.4 1.8 fusion.191
  135.9 2.3 fusion.59
  143.1 1.5 collective-permute-start.16
  144.6 1.5 pad_maximum_fusion.8
  151.8 1.9 collective-permute-start.15
  156.9 3.0 fusion.134
  165.6 5.4 %collective-permute-start.17 = (f32[2,2,1024]{2,0,1:T(2,128)S(1)}, f32[2,2,1024]{2,0,1:T(2,128)}, u32[]{:S(2)}, u32[]{:S(2)}) collective-permute-start(f32[2,2,1024]{2,0,1:T(2,128)S(1)} %pad_maximum_fusion.26), channel_id=1, source_target_pairs={{0,1},{1,2},{2,3},{3,4},{4,5},{5,6},{6,7},{7,8},{8,9},{9,10},{10,1... | collective-permute-start | bytes 49160 | tf_op jit(solution)/shard_map/ppermute | solution.py:16
  171.0 1.4 pad_maximum_fusion.10
  172.5 3.7 %collective-permute-start.19 = (f32[2,2,1,4096]{3,1,2,0:T(2,128)}, f32[2,2,1,4096]{3,1,2,0:T(2,128)}, u32[]{:S(2)}, u32[]{:S(2)}) collective-permute-start(f32[2,2,1,4096]{3,1,2,0:T(2,128)} %pad_maximum_fusion.10), channel_id=1, source_target_pairs={{0,16},{16,32},{32,48},{48,64},{64,80},{80,96},{96,112},{1,17},{17... | collective-permute-start | bytes 196616 | tf_op jit(solution)/shard_map/ppermute | solution.py:16
  179.3 6.6 %fusion.166 = (f32[16,4096]{1,0:T(8,128)}, f32[2,16,4096]{2,1,0:T(8,128)S(1)}, f32[2,16,4096]{2,1,0:T(8,128)S(1)}, f32[2,16,4096]{2,1,0:T(8,128)S(1)}) fusion(f32[2,16,4096]{2,1,0:T(8,128)} %get-tuple-element.35, f32[2,16,4096]{2,1,0:T(8,128)} %copy-done.53, f32[2,16,4096]{2,1,0:T(8,128)S(1)} %get-tuple-element.34, f32[2,16,4096]{2,1,0:T(8,128)} %copy-done.55, ...), kind=kLoop, calls=%fused_computation.172 | loop fusion | flops 7536640 | bytes 14716440 | tf_op jit(solution)/shard_map/reduce_sum | solution.py:153
  189.4 1.9 slice.1112
  191.3 2.1 slice.1116
  193.3 2.0 slice.1120
  198.3 1.9 collective-permute-start.20
  202.5 4.1 %fusion.142 = (f32[2,16,4096]{2,1,0:T(8,128)S(1)}, f32[2,16,4096]{2,1,0:T(8,128)}, f32[2,16,4096]{2,1,0:T(8,128)S(1)}) fusion(f32[2,16,4096]{2,1,0:T(8,128)} %copy-done.42, f32[2,16,4096]{2,1,0:T(8,128)} %copy-done.38, f32[2,16,4096]{2,1,0:T(8,128)} %copy-done.24, f32[2,16,64]{2,1,0:T(8,128)S(1)} %get-tuple-element.100, f32[2,16,4032]{2,1,0:T(8,128)} %slice.1120, ...), kind=kLoop, calls=%fused_computation.148 | loop fusion | flops 3014656 | bytes 7900928 | tf_op jit(solution)/shard_map/sub | solution.py:48
  207.8 6.7 %collective-permute-start.22 = (f32[2,2,1024]{2,0,1:T(2,128)S(1)}, f32[2,2,1024]{2,0,1:T(2,128)}, u32[]{:S(2)}, u32[]{:S(2)}) collective-permute-start(f32[2,2,1024]{2,0,1:T(2,128)S(1)} %pad_maximum_fusion.28), channel_id=1, source_target_pairs={{0,1},{1,2},{2,3},{3,4},{4,5},{5,6},{6,7},{7,8},{8,9},{9,10},{10,1... | collective-permute-start | bytes 49160 | tf_op jit(solution)/shard_map/ppermute | solution.py:16
  216.2 3.6 %collective-permute-start.23 = (f32[2,2,1,4096]{3,1,2,0:T(2,128)}, f32[2,2,1,4096]{3,1,2,0:T(2,128)S(1)}, u32[]{:S(2)}, u32[]{:S(2)}) collective-permute-start(f32[2,2,1,4096]{3,1,2,0:T(2,128)} %pad_maximum_fusion.12), channel_id=1, source_target_pairs={{0,16},{16,32},{32,48},{48,64},{64,80},{80,96},{96,112},{1,17},{17... | collective-permute-start | bytes 196616 | tf_op jit(solution)/shard_map/ppermute | solution.py:16
  222.0 1.9 fusion.209
  228.6 1.9 slice.1140
  230.5 2.1 slice.1144
  232.5 2.0 slice.1150
  237.5 1.9 collective-permute-start.24
  241.7 4.1 %fusion.150 = (f32[2,16,4096]{2,1,0:T(8,128)S(1)}, f32[2,16,4096]{2,1,0:T(8,128)}, f32[2,16,4096]{2,1,0:T(8,128)S(1)}) fusion(f32[2,16,4096]{2,1,0:T(8,128)} %copy-done.10, f32[2,16,4096]{2,1,0:T(8,128)} %copy-done.41, f32[2,16,4096]{2,1,0:T(8,128)} %copy-done.22, f32[2,16,64]{2,1,0:T(8,128)S(1)} %get-tuple-element.96, f32[2,16,4032]{2,1,0:T(8,128)} %slice.1148, ...), kind=kLoop, calls=%fused_computation.156 | loop fusion | flops 3014656 | bytes 7900928 | tf_op jit(solution)/shard_map/sub | solution.py:48
  247.0 6.7 %collective-permute-start.26 = (f32[2,2,1024]{2,0,1:T(2,128)S(1)}, f32[2,2,1024]{2,0,1:T(2,128)}, u32[]{:S(2)}, u32[]{:S(2)}) collective-permute-start(f32[2,2,1024]{2,0,1:T(2,128)S(1)} %pad_maximum_fusion.30), channel_id=1, source_target_pairs={{0,1},{1,2},{2,3},{3,4},{4,5},{5,6},{6,7},{7,8},{8,9},{9,10},{10,1... | collective-permute-start | bytes 49160 | tf_op jit(solution)/shard_map/ppermute | solution.py:16
  255.4 3.6 %collective-permute-start.27 = (f32[2,2,1,4096]{3,1,2,0:T(2,128)}, f32[2,2,1,4096]{3,1,2,0:T(2,128)S(1)}, u32[]{:S(2)}, u32[]{:S(2)}) collective-permute-start(f32[2,2,1,4096]{3,1,2,0:T(2,128)} %pad_maximum_fusion.14), channel_id=1, source_target_pairs={{0,16},{16,32},{32,48},{48,64},{64,80},{80,96},{96,112},{1,17},{17... | collective-permute-start | bytes 196616 | tf_op jit(solution)/shard_map/ppermute | solution.py:16
  261.2 5.6 %add_reduce_fusion.1 = (f32[16,4096]{1,0:T(8,128)}, f32[16,4096]{1,0:T(8,128)}, f32[2,16,4096]{2,1,0:T(8,128)S(1)}, f32[2,16,4096]{2,1,0:T(8,128)S(1)}, f32[2,16,4096]{2,1,0:T(8,128)S(1)}) fusion(f32[2,16,4096]{2,1,0:T(8,128)} %copy-done.22, f32[2,16,4096]{2,1,0:T(8,128)S(1)} %fusion.191, f32[2,16,4096]{2,1,0:T(8,128)S(1)} %fusion.184, ...), kind=kLoop, calls=%fused_computation.295 | loop fusion | flops 5242880 | bytes 13405952 | tf_op jit(solution)/shard_map/reduce_sum | solution.py:153
  269.7 2.0 slice.1168
  271.7 2.1 slice.1172
  273.8 2.0 slice.1176
  278.6 1.9 collective-permute-start.28
  283.4 2.8 fusion.158
  287.7 6.1 %collective-permute-start.30 = (f32[2,2,1024]{2,0,1:T(2,128)S(1)}, f32[2,2,1024]{2,0,1:T(2,128)S(1)}, u32[]{:S(2)}, u32[]{:S(2)}) collective-permute-start(f32[2,2,1024]{2,0,1:T(2,128)S(1)} %pad_maximum_fusion.32), channel_id=1, source_target_pairs={{0,1},{1,2},{2,3},{3,4},{4,5},{5,6},{6,7},{7,8},{8,9},{9,10},{10,1... | collective-permute-start | bytes 49160 | tf_op jit(solution)/shard_map/ppermute | solution.py:16
  293.8 4.0 %collective-permute-start.31 = (f32[2,2,1,4096]{3,1,2,0:T(2,128)S(1)}, f32[2,2,1,4096]{3,1,2,0:T(2,128)S(1)}, u32[]{:S(2)}, u32[]{:S(2)}) collective-permute-start(f32[2,2,1,4096]{3,1,2,0:T(2,128)S(1)} %pad_maximum_fusion.16), channel_id=1, source_target_pairs={{0,16},{16,32},{32,48},{48,64},{64,80},{80,96},{96,112},{1,17},{17... | collective-permute-start | bytes 196616 | tf_op jit(solution)/shard_map/ppermute | solution.py:16
  299.5 4.2 %fusion.93 = f32[16,4096]{1,0:T(8,128)S(1)} fusion(f32[2,16,4096]{2,1,0:T(8,128)} %copy-done.44, f32[2,16,4096]{2,1,0:T(8,128)} %copy-done.54, f32[2,16,4096]{2,1,0:T(8,128)} %copy-done.36, f32[2,16,4096]{2,1,0:T(8,128)} %copy-done.56, f32[2,16,4096]{2,1,0:T(8,128)} %copy-done.52, f32[2,16,4032]{2,1,0:T(8,128)} %bitcast.417, ...), kind=kLoop, calls=%fused_computation.99 | loop fusion | flops 4128768 | bytes 9998080 | tf_op jit(solution)/shard_map/reduce_sum | solution.py:153
  306.0 17.4 %all_to_all.10 = f32[2,16,4,1,512]{4,2,1,3,0:T(4,128)S(1)} all-to-all(f32[2,16,4,1,512]{4,2,1,3,0:T(4,128)S(1)} %pad_maximum_fusion), channel_id=1, replica_groups=mesh['src'=2,'gx'=8,'gy'=16] {'src'}, dimensions={0} | all-to-all | bytes 524288 | tf_op jit(solution)/shard_map/all_to_all | solution.py:174
  324.1 15.0 %all-to-all-start.1 = ((f32[16,4,2,512]{3,1,2,0:T(4,128)}), f32[16,4,2,512]{3,1,2,0:T(4,128)S(1)}, u32[]{:S(2)}, u32[]{:S(2)}) async-start(f32[16,4,2,512]{3,1,2,0:T(4,128)} %copy.57), calls=%async_computation.1 | async-start | bytes 524288 | tf_op jit(solution)/shard_map/all_to_all | solution.py:172
  339.1 8.7 %all-to-all-done.1 = f32[16,4,2,512]{3,1,2,0:T(4,128)S(1)} async-done(((f32[16,4,2,512]{3,1,2,0:T(4,128)}), f32[16,4,2,512]{3,1,2,0:T(4,128)S(1)}, u32[]{:S(2)}, u32[]{:S(2)}) %all-to-all-start.1) | async-done | bytes 262176 | tf_op jit(solution)/shard_map/all_to_all | solution.py:172
  (448 shorter events, 129.3 us)
Async XLA Ops:
  0.0 8.1 %copy-start.16 = (f32[2,6,16,4096]{3,2,1,0:T(8,128)S(1)}, f32[2,6,16,4096]{3,2,1,0:T(8,128)}, u32[]{:S(2)}) copy-start(f32[2,6,16,4096]{3,2,1,0:T(8,128)} %param.9) | copy-start | bytes 9437188
  0.0 16.7 %copy-start.75 = (f32[16,4096]{1,0:T(8,128)S(1)}, f32[16,4096]{1,0:T(8,128)}, u32[]{:S(2)}) copy-start(f32[16,4096]{1,0:T(8,128)} %param.10) | copy-start | bytes 786436
  0.0 16.7 %copy-start.79 = (f32[2,4]{1,0:T(2,128)S(1)}, f32[2,4]{1,0:T(2,128)}, u32[]{:S(2)}) copy-start(f32[2,4]{1,0:T(2,128)} %param.11) | copy-start | bytes 100
  0.0 17.5 %copy-start.84 = (s32[4,16]{1,0:T(4,128)S(1)}, s32[4,16]{1,0:T(4,128)}, u32[]{:S(2)}) copy-start(s32[4,16]{1,0:T(4,128)} %param.13) | copy-start | bytes 772
  0.0 17.5 %copy-start.83 = (s32[4,16]{1,0:T(4,128)S(1)}, s32[4,16]{1,0:T(4,128)}, u32[]{:S(2)}) copy-start(s32[4,16]{1,0:T(4,128)} %param.14) | copy-start | bytes 772
  0.0 18.1 %copy-start.82 = (s32[2,3]{1,0:T(2,128)S(1)}, s32[2,3]{1,0:T(2,128)}, u32[]{:S(2)}) copy-start(s32[2,3]{1,0:T(2,128)} %param.12) | copy-start | bytes 76
  4.0 30.5 %collective-permute-start.3 = (f32[2,2,1,4096]{3,1,2,0:T(2,128)}, f32[2,2,1,4096]{3,1,2,0:T(2,128)}, u32[]{:S(2)}, u32[]{:S(2)}) collective-permute-start(f32[2,2,1,4096]{3,1,2,0:T(2,128)} %pad_maximum_fusion.2), channel_id=1, source_target_pairs={{16,0},{32,16},{48,32},{64,48},{80,64},{96,80},{112,96},{17,1},{33... | collective-permute-start | bytes 196616 | tf_op jit(solution)/shard_map/ppermute | solution.py:16
  6.8 26.3 %collective-permute-start.4 = (f32[2,2,1024]{2,0,1:T(2,128)S(1)}, f32[2,2,1024]{2,0,1:T(2,128)S(1)}, u32[]{:S(2)}, u32[]{:S(2)}) collective-permute-start(f32[2,2,1024]{2,0,1:T(2,128)S(1)} %pad_maximum_fusion.19), channel_id=1, source_target_pairs={{1,0},{2,1},{3,2},{4,3},{5,4},{6,5},{7,6},{8,7},{9,8},{10,9},{11,1... | collective-permute-start | bytes 49160 | tf_op jit(solution)/shard_map/ppermute | solution.py:16
  9.0 13.3 %copy-start.61 = (f32[2,16,4096]{2,1,0:T(8,128)S(1)}, f32[2,16,4096]{2,1,0:T(8,128)}, u32[]{:S(2)}) copy-start(f32[2,16,4096]{2,1,0:T(8,128)} %copy-done.60) | copy-start | bytes 1572868
  9.0 17.2 %copy-start.64 = (f32[2,16,4096]{2,1,0:T(8,128)S(1)}, f32[2,16,4096]{2,1,0:T(8,128)}, u32[]{:S(2)}) copy-start(f32[2,16,4096]{2,1,0:T(8,128)} %get-tuple-element.29) | copy-start | bytes 1572868
  10.6 27.7 %collective-permute-start = (f32[2,2,1,4096]{3,1,2,0:T(2,128)}, f32[2,2,1,4096]{3,1,2,0:T(2,128)}, u32[]{:S(2)}, u32[]{:S(2)}) collective-permute-start(f32[2,2,1,4096]{3,1,2,0:T(2,128)} %pad_maximum_fusion.1), channel_id=1, source_target_pairs={{16,0},{32,16},{48,32},{64,48},{80,64},{96,80},{112,96},{17,1},{33... | collective-permute-start | bytes 196616 | tf_op jit(solution)/shard_map/ppermute | solution.py:16
  15.3 18.5 %collective-permute-start.1 = (f32[2,2,1024]{2,0,1:T(2,128)S(1)}, f32[2,2,1024]{2,0,1:T(2,128)S(1)}, u32[]{:S(2)}, u32[]{:S(2)}) collective-permute-start(f32[2,2,1024]{2,0,1:T(2,128)S(1)} %pad_maximum_fusion.17), channel_id=1, source_target_pairs={{1,0},{2,1},{3,2},{4,3},{5,4},{6,5},{7,6},{8,7},{9,8},{10,9},{11,1... | collective-permute-start | bytes 49160 | tf_op jit(solution)/shard_map/ppermute | solution.py:16
  18.3 76.3 %copy-start.80 = (s32[2]{0:T(128)}, s32[2]{0:T(128)S(1)}, u32[]{:S(2)}) copy-start(s32[2]{0:T(128)S(1)} %get-tuple-element.12) | copy-start | bytes 28
  18.3 9.0 %copy-start.59 = (f32[2,16,4096]{2,1,0:T(8,128)S(1)}, f32[2,16,4096]{2,1,0:T(8,128)}, u32[]{:S(2)}) copy-start(f32[2,16,4096]{2,1,0:T(8,128)} %copy-done.58) | copy-start | bytes 1572868
  44.7 17.9 %collective-permute-start.5 = (f32[2,2,1024]{2,0,1:T(2,128)S(1)}, f32[2,2,1024]{2,0,1:T(2,128)S(1)}, u32[]{:S(2)}, u32[]{:S(2)}) collective-permute-start(f32[2,2,1024]{2,0,1:T(2,128)S(1)} %pad_maximum_fusion.20), channel_id=1, source_target_pairs={{0,1},{1,2},{2,3},{3,4},{4,5},{5,6},{6,7},{7,8},{8,9},{9,10},{10,1... | collective-permute-start | bytes 49160 | tf_op jit(solution)/shard_map/ppermute | solution.py:16
  49.6 9.0 %copy-start.78 = (f32[2,16,64]{2,1,0:T(8,128)S(1)}, f32[2,16,64]{2,1,0:T(8,128)}, u32[]{:S(2)}) copy-start(f32[2,16,64]{2,1,0:T(8,128)} %slice.984) | copy-start | bytes 24580
  50.6 14.1 %collective-permute-start.6 = (f32[2,2,1,4096]{3,1,2,0:T(2,128)S(1)}, f32[2,2,1,4096]{3,1,2,0:T(2,128)S(1)}, u32[]{:S(2)}, u32[]{:S(2)}) collective-permute-start(f32[2,2,1,4096]{3,1,2,0:T(2,128)S(1)} %pad_maximum_fusion.3), channel_id=1, source_target_pairs={{0,16},{16,32},{32,48},{48,64},{64,80},{80,96},{96,112},{1,17},{17... | collective-permute-start | bytes 196616 | tf_op jit(solution)/shard_map/ppermute | solution.py:16
  52.6 12.2 %copy-start.4 = (f32[2,16,4096]{2,1,0:T(8,128)S(1)}, f32[2,16,4096]{2,1,0:T(8,128)}, u32[]{:S(2)}) copy-start(f32[2,16,4096]{2,1,0:T(8,128)} %get-tuple-element.25) | copy-start | bytes 1572868
  52.6 12.2 %copy-start.9 = (f32[2,16,4096]{2,1,0:T(8,128)S(1)}, f32[2,16,4096]{2,1,0:T(8,128)}, u32[]{:S(2)}) copy-start(f32[2,16,4096]{2,1,0:T(8,128)} %copy-done.8) | copy-start | bytes 1572868
  52.6 12.2 %copy-start.87 = (f32[2]{0:T(128)S(1)}, f32[2]{0:T(128)}, u32[]{:S(2)}) copy-start(f32[2]{0:T(128)} %get-tuple-element.9) | copy-start | bytes 28
  55.4 9.4 %copy-start.34 = (f32[2,16,4096]{2,1,0:T(8,128)}, f32[2,16,4096]{2,1,0:T(8,128)S(1)}, u32[]{:S(2)}) copy-start(f32[2,16,4096]{2,1,0:T(8,128)S(1)} %get-tuple-element.23) | copy-start | bytes 1572868
  55.4 10.8 %copy-start.42 = (f32[2,16,4096]{2,1,0:T(8,128)}, f32[2,16,4096]{2,1,0:T(8,128)S(1)}, u32[]{:S(2)}) copy-start(f32[2,16,4096]{2,1,0:T(8,128)S(1)} %get-tuple-element.22) | copy-start | bytes 1572868
  55.4 10.8 %copy-start.27 = (f32[2,16,4096]{2,1,0:T(8,128)S(1)}, f32[2,16,4096]{2,1,0:T(8,128)}, u32[]{:S(2)}) copy-start(f32[2,16,4096]{2,1,0:T(8,128)} %copy-done.26) | copy-start | bytes 1572868
  56.1 13.3 %collective-permute-start.18 = (f32[2,2,1,4096]{3,1,2,0:T(2,128)}, f32[2,2,1,4096]{3,1,2,0:T(2,128)}, u32[]{:S(2)}, u32[]{:S(2)}) collective-permute-start(f32[2,2,1,4096]{3,1,2,0:T(2,128)} %pad_maximum_fusion.9), channel_id=1, source_target_pairs={{0,16},{16,32},{32,48},{48,64},{64,80},{80,96},{96,112},{1,17},{17... | collective-permute-start | bytes 196616 | tf_op jit(solution)/shard_map/ppermute | solution.py:16
  58.7 5.4 %collective-permute-start.2 = (f32[2,2,1024]{2,0,1:T(2,128)S(1)}, f32[2,2,1024]{2,0,1:T(2,128)S(1)}, u32[]{:S(2)}, u32[]{:S(2)}) collective-permute-start(f32[2,2,1024]{2,0,1:T(2,128)S(1)} %pad_maximum_fusion.18), channel_id=1, source_target_pairs={{0,1},{1,2},{2,3},{3,4},{4,5},{5,6},{6,7},{7,8},{8,9},{9,10},{10,1... | collective-permute-start | bytes 49160 | tf_op jit(solution)/shard_map/ppermute | solution.py:16
  68.1 10.5 %collective-permute-start.8 = (f32[2,2,1024]{2,0,1:T(2,128)S(1)}, f32[2,2,1024]{2,0,1:T(2,128)S(1)}, u32[]{:S(2)}, u32[]{:S(2)}) collective-permute-start(f32[2,2,1024]{2,0,1:T(2,128)S(1)} %pad_maximum_fusion.21), channel_id=1, source_target_pairs={{1,0},{2,1},{3,2},{4,3},{5,4},{6,5},{7,6},{8,7},{9,8},{10,9},{11,1... | collective-permute-start | bytes 49160 | tf_op jit(solution)/shard_map/ppermute | solution.py:16
  76.2 4.3 %collective-permute-start.7 = (f32[2,2,1,4096]{3,1,2,0:T(2,128)S(1)}, f32[2,2,1,4096]{3,1,2,0:T(2,128)S(1)}, u32[]{:S(2)}, u32[]{:S(2)}) collective-permute-start(f32[2,2,1,4096]{3,1,2,0:T(2,128)S(1)} %pad_maximum_fusion.4), channel_id=1, source_target_pairs={{16,0},{32,16},{48,32},{64,48},{80,64},{96,80},{112,96},{17,1},{33... | collective-permute-start | bytes 196616 | tf_op jit(solution)/shard_map/ppermute | solution.py:16
  80.6 14.0 %copy-start.86 = (f32[2]{0:T(128)S(1)}, f32[2]{0:T(128)}, u32[]{:S(2)}) copy-start(f32[2]{0:T(128)} %get-tuple-element.8) | copy-start | bytes 28
  84.3 8.2 %collective-permute-start.9 = (f32[2,2,1024]{2,0,1:T(2,128)S(1)}, f32[2,2,1024]{2,0,1:T(2,128)S(1)}, u32[]{:S(2)}, u32[]{:S(2)}) collective-permute-start(f32[2,2,1024]{2,0,1:T(2,128)S(1)} %pad_maximum_fusion.22), channel_id=1, source_target_pairs={{0,1},{1,2},{2,3},{3,4},{4,5},{5,6},{6,7},{7,8},{8,9},{9,10},{10,1... | collective-permute-start | bytes 49160 | tf_op jit(solution)/shard_map/ppermute | solution.py:16
  88.9 5.6 %collective-permute-start.10 = (f32[2,2,1,4096]{3,1,2,0:T(2,128)S(1)}, f32[2,2,1,4096]{3,1,2,0:T(2,128)S(1)}, u32[]{:S(2)}, u32[]{:S(2)}) collective-permute-start(f32[2,2,1,4096]{3,1,2,0:T(2,128)S(1)} %pad_maximum_fusion.5), channel_id=1, source_target_pairs={{0,16},{16,32},{32,48},{48,64},{64,80},{80,96},{96,112},{1,17},{17... | collective-permute-start | bytes 196616 | tf_op jit(solution)/shard_map/ppermute | solution.py:16
  98.0 18.6 %copy-start.1 = (f32[2,16,4096]{2,1,0:T(8,128)}, f32[2,16,4096]{2,1,0:T(8,128)S(1)}, u32[]{:S(2)}) copy-start(f32[2,16,4096]{2,1,0:T(8,128)S(1)} %get-tuple-element.36) | copy-start | bytes 1572868
  103.0 10.5 %collective-permute-start.12 = (f32[2,2,1024]{2,0,1:T(2,128)S(1)}, f32[2,2,1024]{2,0,1:T(2,128)}, u32[]{:S(2)}, u32[]{:S(2)}) collective-permute-start(f32[2,2,1024]{2,0,1:T(2,128)S(1)} %pad_maximum_fusion.23), channel_id=1, source_target_pairs={{1,0},{2,1},{3,2},{4,3},{5,4},{6,5},{7,6},{8,7},{9,8},{10,9},{11,1... | collective-permute-start | bytes 49160 | tf_op jit(solution)/shard_map/ppermute | solution.py:16
  111.5 4.1 %collective-permute-start.11 = (f32[2,2,1,4096]{3,1,2,0:T(2,128)}, f32[2,2,1,4096]{3,1,2,0:T(2,128)}, u32[]{:S(2)}, u32[]{:S(2)}) collective-permute-start(f32[2,2,1,4096]{3,1,2,0:T(2,128)} %pad_maximum_fusion.6), channel_id=1, source_target_pairs={{16,0},{32,16},{48,32},{64,48},{80,64},{96,80},{112,96},{17,1},{33... | collective-permute-start | bytes 196616 | tf_op jit(solution)/shard_map/ppermute | solution.py:16
  116.6 16.7 %copy-start.81 = (s32[2]{0:T(128)S(1)}, s32[2]{0:T(128)}, u32[]{:S(2)}) copy-start(s32[2]{0:T(128)} %copy-done.80) | copy-start | bytes 28
  116.6 16.7 %copy-start.85 = (f32[2]{0:T(128)S(1)}, f32[2]{0:T(128)}, u32[]{:S(2)}) copy-start(f32[2]{0:T(128)} %get-tuple-element.10) | copy-start | bytes 28
  121.5 9.9 %collective-permute-start.13 = (f32[2,2,1024]{2,0,1:T(2,128)S(1)}, f32[2,2,1024]{2,0,1:T(2,128)S(1)}, u32[]{:S(2)}, u32[]{:S(2)}) collective-permute-start(f32[2,2,1024]{2,0,1:T(2,128)S(1)} %pad_maximum_fusion.24), channel_id=1, source_target_pairs={{0,1},{1,2},{2,3},{3,4},{4,5},{5,6},{6,7},{7,8},{8,9},{9,10},{10,1... | collective-permute-start | bytes 49160 | tf_op jit(solution)/shard_map/ppermute | solution.py:16
  127.7 5.6 %collective-permute-start.14 = (f32[2,2,1,4096]{3,1,2,0:T(2,128)S(1)}, f32[2,2,1,4096]{3,1,2,0:T(2,128)S(1)}, u32[]{:S(2)}, u32[]{:S(2)}) collective-permute-start(f32[2,2,1,4096]{3,1,2,0:T(2,128)S(1)} %pad_maximum_fusion.7), channel_id=1, source_target_pairs={{0,16},{16,32},{32,48},{48,64},{64,80},{80,96},{96,112},{1,17},{17... | collective-permute-start | bytes 196616 | tf_op jit(solution)/shard_map/ppermute | solution.py:16
  143.1 10.6 %collective-permute-start.16 = (f32[2,2,1024]{2,0,1:T(2,128)S(1)}, f32[2,2,1024]{2,0,1:T(2,128)}, u32[]{:S(2)}, u32[]{:S(2)}) collective-permute-start(f32[2,2,1024]{2,0,1:T(2,128)S(1)} %pad_maximum_fusion.25), channel_id=1, source_target_pairs={{1,0},{2,1},{3,2},{4,3},{5,4},{6,5},{7,6},{8,7},{9,8},{10,9},{11,1... | collective-permute-start | bytes 49160 | tf_op jit(solution)/shard_map/ppermute | solution.py:16
  151.8 4.1 %collective-permute-start.15 = (f32[2,2,1,4096]{3,1,2,0:T(2,128)}, f32[2,2,1,4096]{3,1,2,0:T(2,128)}, u32[]{:S(2)}, u32[]{:S(2)}) collective-permute-start(f32[2,2,1,4096]{3,1,2,0:T(2,128)} %pad_maximum_fusion.8), channel_id=1, source_target_pairs={{16,0},{32,16},{48,32},{64,48},{80,64},{96,80},{112,96},{17,1},{33... | collective-permute-start | bytes 196616 | tf_op jit(solution)/shard_map/ppermute | solution.py:16
  165.6 10.6 %collective-permute-start.17 = (f32[2,2,1024]{2,0,1:T(2,128)S(1)}, f32[2,2,1024]{2,0,1:T(2,128)}, u32[]{:S(2)}, u32[]{:S(2)}) collective-permute-start(f32[2,2,1024]{2,0,1:T(2,128)S(1)} %pad_maximum_fusion.26), channel_id=1, source_target_pairs={{0,1},{1,2},{2,3},{3,4},{4,5},{5,6},{6,7},{7,8},{8,9},{9,10},{10,1... | collective-permute-start | bytes 49160 | tf_op jit(solution)/shard_map/ppermute | solution.py:16
  172.5 5.9 %collective-permute-start.19 = (f32[2,2,1,4096]{3,1,2,0:T(2,128)}, f32[2,2,1,4096]{3,1,2,0:T(2,128)}, u32[]{:S(2)}, u32[]{:S(2)}) collective-permute-start(f32[2,2,1,4096]{3,1,2,0:T(2,128)} %pad_maximum_fusion.10), channel_id=1, source_target_pairs={{0,16},{16,32},{32,48},{48,64},{64,80},{80,96},{96,112},{1,17},{17... | collective-permute-start | bytes 196616 | tf_op jit(solution)/shard_map/ppermute | solution.py:16
  187.2 8.1 %copy-start.39 = (f32[2,16,4096]{2,1,0:T(8,128)S(1)}, f32[2,16,4096]{2,1,0:T(8,128)}, u32[]{:S(2)}) copy-start(f32[2,16,4096]{2,1,0:T(8,128)} %copy-done.38) | copy-start | bytes 1572868
  187.2 9.2 %copy-start.47 = (f32[2,16,4096]{2,1,0:T(8,128)S(1)}, f32[2,16,4096]{2,1,0:T(8,128)}, u32[]{:S(2)}) copy-start(f32[2,16,4096]{2,1,0:T(8,128)} %copy-done.46) | copy-start | bytes 1572868
  187.2 10.2 %copy-start.25 = (f32[2,16,4096]{2,1,0:T(8,128)S(1)}, f32[2,16,4096]{2,1,0:T(8,128)}, u32[]{:S(2)}) copy-start(f32[2,16,4096]{2,1,0:T(8,128)} %copy-done.24) | copy-start | bytes 1572868
  187.3 13.0 %collective-permute-start.21 = (f32[2,2,1024]{2,0,1:T(2,128)S(1)}, f32[2,2,1024]{2,0,1:T(2,128)}, u32[]{:S(2)}, u32[]{:S(2)}) collective-permute-start(f32[2,2,1024]{2,0,1:T(2,128)S(1)} %pad_maximum_fusion.27), channel_id=1, source_target_pairs={{1,0},{2,1},{3,2},{4,3},{5,4},{6,5},{7,6},{8,7},{9,8},{10,9},{11,1... | collective-permute-start | bytes 49160 | tf_op jit(solution)/shard_map/ppermute | solution.py:16
  198.3 4.1 %collective-permute-start.20 = (f32[2,2,1,4096]{3,1,2,0:T(2,128)}, f32[2,2,1,4096]{3,1,2,0:T(2,128)S(1)}, u32[]{:S(2)}, u32[]{:S(2)}) collective-permute-start(f32[2,2,1,4096]{3,1,2,0:T(2,128)} %pad_maximum_fusion.11), channel_id=1, source_target_pairs={{16,0},{32,16},{48,32},{64,48},{80,64},{96,80},{112,96},{17,1},{33... | collective-permute-start | bytes 196616 | tf_op jit(solution)/shard_map/ppermute | solution.py:16
  207.8 11.9 %collective-permute-start.22 = (f32[2,2,1024]{2,0,1:T(2,128)S(1)}, f32[2,2,1024]{2,0,1:T(2,128)}, u32[]{:S(2)}, u32[]{:S(2)}) collective-permute-start(f32[2,2,1024]{2,0,1:T(2,128)S(1)} %pad_maximum_fusion.28), channel_id=1, source_target_pairs={{0,1},{1,2},{2,3},{3,4},{4,5},{5,6},{6,7},{7,8},{8,9},{9,10},{10,1... | collective-permute-start | bytes 49160 | tf_op jit(solution)/shard_map/ppermute | solution.py:16
  216.2 5.8 %collective-permute-start.23 = (f32[2,2,1,4096]{3,1,2,0:T(2,128)}, f32[2,2,1,4096]{3,1,2,0:T(2,128)S(1)}, u32[]{:S(2)}, u32[]{:S(2)}) collective-permute-start(f32[2,2,1,4096]{3,1,2,0:T(2,128)} %pad_maximum_fusion.12), channel_id=1, source_target_pairs={{0,16},{16,32},{32,48},{48,64},{64,80},{80,96},{96,112},{1,17},{17... | collective-permute-start | bytes 196616 | tf_op jit(solution)/shard_map/ppermute | solution.py:16
  226.5 8.1 %copy-start.50 = (f32[2,16,4096]{2,1,0:T(8,128)S(1)}, f32[2,16,4096]{2,1,0:T(8,128)}, u32[]{:S(2)}) copy-start(f32[2,16,4096]{2,1,0:T(8,128)} %copy-done.49) | copy-start | bytes 1572868
  226.5 9.2 %copy-start.23 = (f32[2,16,4096]{2,1,0:T(8,128)S(1)}, f32[2,16,4096]{2,1,0:T(8,128)}, u32[]{:S(2)}) copy-start(f32[2,16,4096]{2,1,0:T(8,128)} %copy-done.22) | copy-start | bytes 1572868
  226.5 12.9 %collective-permute-start.25 = (f32[2,2,1024]{2,0,1:T(2,128)S(1)}, f32[2,2,1024]{2,0,1:T(2,128)}, u32[]{:S(2)}, u32[]{:S(2)}) collective-permute-start(f32[2,2,1024]{2,0,1:T(2,128)S(1)} %pad_maximum_fusion.29), channel_id=1, source_target_pairs={{1,0},{2,1},{3,2},{4,3},{5,4},{6,5},{7,6},{8,7},{9,8},{10,9},{11,1... | collective-permute-start | bytes 49160 | tf_op jit(solution)/shard_map/ppermute | solution.py:16
  237.5 4.1 %collective-permute-start.24 = (f32[2,2,1,4096]{3,1,2,0:T(2,128)}, f32[2,2,1,4096]{3,1,2,0:T(2,128)S(1)}, u32[]{:S(2)}, u32[]{:S(2)}) collective-permute-start(f32[2,2,1,4096]{3,1,2,0:T(2,128)} %pad_maximum_fusion.13), channel_id=1, source_target_pairs={{16,0},{32,16},{48,32},{64,48},{80,64},{96,80},{112,96},{17,1},{33... | collective-permute-start | bytes 196616 | tf_op jit(solution)/shard_map/ppermute | solution.py:16
  247.0 11.9 %collective-permute-start.26 = (f32[2,2,1024]{2,0,1:T(2,128)S(1)}, f32[2,2,1024]{2,0,1:T(2,128)}, u32[]{:S(2)}, u32[]{:S(2)}) collective-permute-start(f32[2,2,1024]{2,0,1:T(2,128)S(1)} %pad_maximum_fusion.30), channel_id=1, source_target_pairs={{0,1},{1,2},{2,3},{3,4},{4,5},{5,6},{6,7},{7,8},{8,9},{9,10},{10,1... | collective-permute-start | bytes 49160 | tf_op jit(solution)/shard_map/ppermute | solution.py:16
  255.4 5.8 %collective-permute-start.27 = (f32[2,2,1,4096]{3,1,2,0:T(2,128)}, f32[2,2,1,4096]{3,1,2,0:T(2,128)S(1)}, u32[]{:S(2)}, u32[]{:S(2)}) collective-permute-start(f32[2,2,1,4096]{3,1,2,0:T(2,128)} %pad_maximum_fusion.14), channel_id=1, source_target_pairs={{0,16},{16,32},{32,48},{48,64},{64,80},{80,96},{96,112},{1,17},{17... | collective-permute-start | bytes 196616 | tf_op jit(solution)/shard_map/ppermute | solution.py:16
  267.6 10.2 %copy-start.21 = (f32[2,16,4096]{2,1,0:T(8,128)S(1)}, f32[2,16,4096]{2,1,0:T(8,128)}, u32[]{:S(2)}) copy-start(f32[2,16,4096]{2,1,0:T(8,128)} %copy-done.20) | copy-start | bytes 1572868
  268.2 8.6 %copy-start.45 = (f32[2,16,4096]{2,1,0:T(8,128)S(1)}, f32[2,16,4096]{2,1,0:T(8,128)}, u32[]{:S(2)}) copy-start(f32[2,16,4096]{2,1,0:T(8,128)} %copy-done.44) | copy-start | bytes 1572868
  268.2 12.4 %collective-permute-start.29 = (f32[2,2,1024]{2,0,1:T(2,128)S(1)}, f32[2,2,1024]{2,0,1:T(2,128)}, u32[]{:S(2)}, u32[]{:S(2)}) collective-permute-start(f32[2,2,1024]{2,0,1:T(2,128)S(1)} %pad_maximum_fusion.31), channel_id=1, source_target_pairs={{1,0},{2,1},{3,2},{4,3},{5,4},{6,5},{7,6},{8,7},{9,8},{10,9},{11,1... | collective-permute-start | bytes 49160 | tf_op jit(solution)/shard_map/ppermute | solution.py:16
  269.7 13.7 %copy-start.19 = (f32[2,16,4096]{2,1,0:T(8,128)S(1)}, f32[2,16,4096]{2,1,0:T(8,128)}, u32[]{:S(2)}) copy-start(f32[2,16,4096]{2,1,0:T(8,128)} %copy-done.18) | copy-start | bytes 1572868
  269.7 13.7 %copy-start.35 = (f32[2,16,4096]{2,1,0:T(8,128)S(1)}, f32[2,16,4096]{2,1,0:T(8,128)}, u32[]{:S(2)}) copy-start(f32[2,16,4096]{2,1,0:T(8,128)} %get-tuple-element.42) | copy-start | bytes 1572868
  278.6 3.8 %collective-permute-start.28 = (f32[2,2,1,4096]{3,1,2,0:T(2,128)S(1)}, f32[2,2,1,4096]{3,1,2,0:T(2,128)}, u32[]{:S(2)}, u32[]{:S(2)}) collective-permute-start(f32[2,2,1,4096]{3,1,2,0:T(2,128)S(1)} %pad_maximum_fusion.15), channel_id=1, source_target_pairs={{16,0},{32,16},{48,32},{64,48},{80,64},{96,80},{112,96},{17,1},{33... | collective-permute-start | bytes 196616 | tf_op jit(solution)/shard_map/ppermute | solution.py:16
  287.7 10.2 %collective-permute-start.30 = (f32[2,2,1024]{2,0,1:T(2,128)S(1)}, f32[2,2,1024]{2,0,1:T(2,128)S(1)}, u32[]{:S(2)}, u32[]{:S(2)}) collective-permute-start(f32[2,2,1024]{2,0,1:T(2,128)S(1)} %pad_maximum_fusion.32), channel_id=1, source_target_pairs={{0,1},{1,2},{2,3},{3,4},{4,5},{5,6},{6,7},{7,8},{8,9},{9,10},{10,1... | collective-permute-start | bytes 49160 | tf_op jit(solution)/shard_map/ppermute | solution.py:16
  293.8 5.6 %collective-permute-start.31 = (f32[2,2,1,4096]{3,1,2,0:T(2,128)S(1)}, f32[2,2,1,4096]{3,1,2,0:T(2,128)S(1)}, u32[]{:S(2)}, u32[]{:S(2)}) collective-permute-start(f32[2,2,1,4096]{3,1,2,0:T(2,128)S(1)} %pad_maximum_fusion.16), channel_id=1, source_target_pairs={{0,16},{16,32},{32,48},{48,64},{64,80},{80,96},{96,112},{1,17},{17... | collective-permute-start | bytes 196616 | tf_op jit(solution)/shard_map/ppermute | solution.py:16
  303.9 35.2 %copy-start.88 = (s32[1,64]{1,0:T(1,128)S(1)}, s32[1,64]{1,0:T(1,128)}, u32[]{:S(2)}) copy-start(s32[1,64]{1,0:T(1,128)} %param.15) | copy-start | bytes 772
  324.1 23.7 %all-to-all-start.1 = ((f32[16,4,2,512]{3,1,2,0:T(4,128)}), f32[16,4,2,512]{3,1,2,0:T(4,128)S(1)}, u32[]{:S(2)}, u32[]{:S(2)}) async-start(f32[16,4,2,512]{3,1,2,0:T(4,128)} %copy.57), calls=%async_computation.1 | async-start | bytes 524288 | tf_op jit(solution)/shard_map/all_to_all | solution.py:172
  (58 other events, 182.2 us)
